TPU v7x, 256 devices: a whole 4x4x8 slice. The times are simulated.
256 devices in a mesh: seq: 64 (over y, z_hi, x), head: 4 (over z_lo, core).
Axes of the slice: x: 4, y: 4, z: 8 (z_hi: 4, z_lo: 2; z = z_hi * 2 + z_lo), core: 2. Of those that a mesh axis runs over, the one named last changes fastest.
Arguments:
- inputs: bfloat16 [256, 512, 768], P('seq'), may hold values from -6 to 6
- out_grad: bfloat16 [256, 512, 768], P('seq'), may hold values from -16 to 16
- w_query: bfloat16 [768, 512], P(None, 'head'), may hold values from -0.21875 to 0.21875
- w_key: bfloat16 [768, 512], P(None, 'head'), may hold values from -0.21875 to 0.21875
- w_value: bfloat16 [768, 512], P(None, 'head'), may hold values from -0.21875 to 0.21875
- w_output: bfloat16 [512, 768], P('head'), may hold values from -0.25 to 0.25
Outputs:
- grad_inputs: bfloat16 [256, 512, 768], P('seq', 'head')
- grad_wq: float32 [768, 512], P(None, 'head')
- grad_wk: float32 [768, 512], P(None, 'head')
- grad_wv: float32 [768, 512], P(None, 'head')
- grad_wo: float32 [512, 768], P('head')
All inputs are finite; a program needn't handle non-finite values.
Results may differ from a plain program's by a relative error of at most 0.012.
Values may be sent and summed in bfloat16 or wider, within the bound.
A program may use at most 64 MiB of HBM per device.

v0:
```python
import math

import jax
import jax.numpy as jnp
from jax import lax
from jax.sharding import Mesh
from jax.sharding import PartitionSpec as P

HEAD_DIM = 64
HEAD = ("head_0", "head_1")


def from_everyone(value, axis):
    count = lax.axis_size(axis)
    return lax.all_to_all(
        jnp.broadcast_to(value[None], (count, *value.shape)), axis, 0, 0, tiled=True
    )


def laid_out(blocks, dim):
    dims = list(blocks.shape[1:])
    dims[dim] *= blocks.shape[0]
    return jnp.moveaxis(blocks, 0, dim).reshape(dims)


def gather_axes(value, axes, dim):
    far, near = axes
    blocks = from_everyone(from_everyone(value, far), near)
    return laid_out(blocks.swapaxes(0, 1).reshape(-1, *value.shape), dim)


def in_one_piece(arrays, axis, dim, along):
    widths = [a.shape[along] for a in arrays]
    both = jnp.concatenate(arrays, axis=along)
    whole = gather_axes(both, axis, dim)
    return tuple(jnp.split(whole, [sum(widths[:k]) for k in range(1, len(widths))], axis=along))


def in_blocks(value, dim, count):
    before, after = (value.shape[:dim], value.shape[dim + 1 :])
    return jnp.moveaxis(value.reshape(*before, count, -1, *after), dim, 0)


def sum_at_owner(value, axis, dim):
    count = lax.axis_size(axis)
    blocks = lax.all_to_all(in_blocks(value, dim, count), axis, 0, 0, tiled=True)
    return jnp.sum(blocks.astype(jnp.float32), axis=0)


def sent_together(arrays, axis, dim, along):
    ends, at = ([], 0)
    for a in arrays[:-1]:
        at += a.shape[along]
        ends.append(at)
    both = jnp.concatenate(arrays, axis=along)
    return tuple(jnp.split(sum_at_owner(both, axis, dim), ends, axis=along))


def side_by_side(arrays, axis, dim, along):
    ends, at = ([], 0)
    for a in arrays[:-1]:
        at += a.shape[along]
        ends.append(at)
    both = jnp.concatenate(arrays, axis=along)
    return tuple(jnp.split(lax.all_gather(both, axis, axis=dim, tiled=True), ends, axis=along))


def side_by_side_2(arrays, axis, split_dim, concat_dim, along):
    widths = [a.shape[along] for a in arrays]
    both = jnp.concatenate(arrays, axis=along)
    whole = lax.all_to_all(both, axis, split_axis=split_dim, concat_axis=concat_dim, tiled=True)
    return tuple(jnp.split(whole, [sum(widths[:k]) for k in range(1, len(widths))], axis=along))


def padded_to(lines, count):
    spare = -lines.shape[0] % count
    if not spare:
        return lines
    return jnp.concatenate([lines, jnp.zeros((spare, *lines.shape[1:]), lines.dtype)])


def gathered_copies(value, axis, dim):
    return laid_out(from_everyone(value, axis), dim)


def nested_sum(value, axes):
    lines = value.reshape(-1, value.shape[-1])
    padded = padded_to(lines, lax.axis_size(axes))
    whole = gathered_copies(sum_at_owner(padded, axes, 0).astype(jnp.bfloat16), axes, 0)
    return lax.slice_in_dim(whole, 0, len(lines)).reshape(value.shape).astype(jnp.float32)


def times_transpose(left, right):
    return lax.dot_general(
        left, right, (((1,), (1,)), ((), ())), preferred_element_type=jnp.float32
    )


def first_contract(left, right):
    return lax.dot_general(
        left, right, (((0,), (0,)), ((), ())), preferred_element_type=jnp.float32
    )


def softmax_rows(logits):
    exponent = jnp.exp(logits)
    attn_probs = exponent / jnp.sum(exponent, axis=2, keepdims=True)
    return (attn_probs, attn_probs.astype(jnp.bfloat16))


def score_grad(attn_probs, grad_probs, logit_scale):
    row_inner = jnp.sum(attn_probs * grad_probs, axis=2, keepdims=True)
    return (logit_scale * attn_probs * (grad_probs - row_inner)).astype(jnp.bfloat16)


def body(inputs, out_grad, w_query, w_key, w_value, w_output):
    row_count, col_count, model_width = inputs.shape
    local_width = w_query.shape[1]
    head_count = local_width // HEAD_DIM
    all_rows = row_count * lax.axis_size("seq")
    logit_scale = 1.0 / (math.sqrt(HEAD_DIM) * math.sqrt(all_rows))
    inv_root = 1.0 / math.sqrt(all_rows * col_count)
    shape_heads = (row_count, col_count, head_count, HEAD_DIM)
    full_query, full_key, full_value = in_one_piece(
        (w_query, w_key, w_value), ("head_0", "head_1"), 1, 0
    )
    flat_in = inputs.reshape(-1, model_width)
    flat_grad = out_grad.reshape(-1, model_width)
    query_proj = jnp.dot(flat_in, w_query, preferred_element_type=jnp.float32).astype(jnp.bfloat16)
    key_proj = jnp.dot(flat_in, w_key, preferred_element_type=jnp.float32).astype(jnp.bfloat16)
    value_proj = jnp.dot(flat_in, w_value, preferred_element_type=jnp.float32).astype(jnp.bfloat16)
    grad_att = times_transpose(flat_grad, w_output).astype(jnp.bfloat16)
    query_four = query_proj.reshape(shape_heads)
    key_four = key_proj.reshape(shape_heads)
    value_four = value_proj.reshape(shape_heads)
    grad_four = grad_att.reshape(shape_heads)
    part_logits = jnp.einsum(
        "rihe,rjhe->hij", query_four, key_four, preferred_element_type=jnp.float32
    )
    part_probs = jnp.einsum(
        "rihe,rjhe->hij", grad_four, value_four, preferred_element_type=jnp.float32
    )
    share_logits, share_grad = sent_together(
        (part_logits.astype(jnp.bfloat16), part_probs.astype(jnp.bfloat16)), "seq", 1, 0
    )
    share_probs, share_low = softmax_rows(logit_scale * share_logits)
    share_dlog = score_grad(share_probs, share_grad, logit_scale)
    probs_low, grad_logits = side_by_side((share_low, share_dlog), "seq", 1, 0)
    attended = jnp.einsum(
        "hij,rjhe->rihe", probs_low, value_four, preferred_element_type=jnp.float32
    )
    attended = attended.astype(jnp.bfloat16).reshape(-1, local_width)
    part_wo = first_contract(attended, flat_grad)
    grad_value = jnp.einsum(
        "hij,rihe->rjhe", probs_low, grad_four, preferred_element_type=jnp.float32
    )
    grad_query = jnp.einsum(
        "hij,rjhe->rihe", grad_logits, key_four, preferred_element_type=jnp.float32
    )
    grad_key = jnp.einsum(
        "hij,rihe->rjhe", grad_logits, query_four, preferred_element_type=jnp.float32
    )
    flat_q = grad_query.astype(jnp.bfloat16).reshape(-1, local_width)
    flat_k = grad_key.astype(jnp.bfloat16).reshape(-1, local_width)
    flat_v = grad_value.astype(jnp.bfloat16).reshape(-1, local_width)
    three_q = flat_q.reshape(row_count, col_count, local_width)
    three_k = flat_k.reshape(row_count, col_count, local_width)
    three_v = flat_v.reshape(row_count, col_count, local_width)
    moved_q, moved_k, moved_v = side_by_side_2((three_q, three_k, three_v), HEAD, 1, 2, 0)
    block_cols = moved_q.shape[1]
    full_width = moved_q.shape[2]
    block_in = times_transpose(moved_q.reshape(-1, full_width), full_query)
    block_in = block_in + times_transpose(moved_k.reshape(-1, full_width), full_key)
    block_in = block_in + times_transpose(moved_v.reshape(-1, full_width), full_value)
    grad_inputs = block_in.astype(jnp.bfloat16).reshape(row_count, block_cols, model_width)
    part_wq = first_contract(flat_in, flat_q)
    part_wk = first_contract(flat_in, flat_k)
    part_wv = first_contract(flat_in, flat_v)
    sum_wq, sum_wk, sum_wv, sum_wo = (
        nested_sum(part_wq.astype(jnp.bfloat16), "seq"),
        nested_sum(part_wk.astype(jnp.bfloat16), "seq"),
        nested_sum(part_wv.astype(jnp.bfloat16), "seq"),
        nested_sum(part_wo.astype(jnp.bfloat16), "seq"),
    )
    return (grad_inputs, sum_wq * inv_root, sum_wk * inv_root, sum_wv * inv_root, sum_wo * inv_root)


def solution(mesh):
    finer = Mesh(mesh.devices.reshape(mesh.shape["seq"], 2, 2), ("seq", "head_0", "head_1"))
    placed = (
        P("seq", None, None),
        P("seq", None, None),
        P(None, HEAD),
        P(None, HEAD),
        P(None, HEAD),
        P(HEAD, None),
    )
    return jax.shard_map(
        body,
        mesh=finer,
        in_specs=placed,
        out_specs=(
            P("seq", HEAD, None),
            P(None, HEAD),
            P(None, HEAD),
            P(None, HEAD),
            P(HEAD, None),
        ),
        check_vma=False,
    )
```

profile of v0, /device:TPU:2, one launch (start us, length us, event | category | flops | bytes accessed | tf_op | source)
XLA Modules:
  0.0 401.8 jit_solution(2369761458171519755)
XLA Ops:
  15.0 3.5 copy.52
  35.5 3.7 convolution_convert_fusion.1
  48.5 67.9 %all_to_all.70 = bf16[64,4,8,512]{3,2,1,0:T(8,128)(2,1)S(1)} all-to-all(bf16[64,4,8,512]{3,2,1,0:T(8,128)(2,1)S(1)} %copy_bitcast_fusion), channel_id=1, replica_groups=mesh['seq'=64,'head_0'=2,'head_1'=2] {'seq'}, dimensions={0} | all-to-all | bytes 4194304 | tf_op jit(solution)/shard_map/all_to_all | solution.py:46
  118.7 15.6 %all_to_all.71 = bf16[2,2304,128]{2,1,0:T(8,128)(2,1)S(1)} all-to-all(bf16[2,2304,128]{2,1,0:T(8,128)(2,1)S(1)} %broadcast_in_dim.12), channel_id=1, replica_groups=mesh['seq'=64,'head_0'=2,'head_1'=2] {'head_0'}, dimensions={0} | all-to-all | bytes 2359296 | tf_op jit(solution)/shard_map/all_to_all | solution.py:15
  136.0 4.9 %all-to-all-start.3 = ((bf16[2,2,2304,128]{3,2,1,0:T(8,128)(2,1)}), bf16[2,2,2304,128]{3,2,1,0:T(8,128)(2,1)}, u32[]{:S(2)}, u32[]{:S(2)}) async-start(bf16[2,2,2304,128]{3,2,1,0:T(8,128)(2,1)} %broadcast_in_dim.13), calls=%async_computation.3 | async-start | bytes 4718592 | tf_op jit(solution)/shard_map/all_to_all | solution.py:15
  140.9 50.6 %all-gather.2.cloned.1.call-done = bf16[4,512,512]{2,1,0:T(8,128)(2,1)} async-done(((bf16[4,8,512]{2,1,0:T(8,128)(2,1)}), bf16[4,512,512]{2,1,0:T(8,128)(2,1)}) %all-gather.2.cloned.1.call-update) | async-done | bytes 2097168 | tf_op jit(solution)/shard_map/all_gather | solution.py:65
  195.4 9.9 %all-to-all-start.10 = ((bf16[64,2,768]{2,1,0:T(2,128)(2,1)}), bf16[64,2,768]{2,1,0:T(2,128)(2,1)S(1)}, u32[]{:S(2)}, u32[]{:S(2)}) async-start(bf16[64,2,768]{2,1,0:T(2,128)(2,1)} %reshape.123), calls=%async_computation.10 | async-start | bytes 393216 | tf_op jit(solution)/shard_map/all_to_all | solution.py:46
  211.6 6.1 %all-to-all-done.10 = bf16[64,2,768]{2,1,0:T(2,128)(2,1)S(1)} async-done(((bf16[64,2,768]{2,1,0:T(2,128)(2,1)}), bf16[64,2,768]{2,1,0:T(2,128)(2,1)S(1)}, u32[]{:S(2)}, u32[]{:S(2)}) %all-to-all-start.10) | async-done | bytes 196640 | tf_op jit(solution)/shard_map/all_to_all | solution.py:46
  218.3 6.7 %all-to-all-start.4 = ((bf16[64,12,128]{2,1,0:T(8,128)(2,1)}), bf16[64,12,128]{2,1,0:T(8,128)(2,1)S(1)}, u32[]{:S(2)}, u32[]{:S(2)}) async-start(bf16[64,12,128]{2,1,0:T(8,128)(2,1)} %reshape.117), calls=%async_computation.4 | async-start | bytes 524288 | tf_op jit(solution)/shard_map/all_to_all | solution.py:46
  232.8 5.2 %all-to-all-done.4 = bf16[64,12,128]{2,1,0:T(8,128)(2,1)S(1)} async-done(((bf16[64,12,128]{2,1,0:T(8,128)(2,1)}), bf16[64,12,128]{2,1,0:T(8,128)(2,1)S(1)}, u32[]{:S(2)}, u32[]{:S(2)}) %all-to-all-start.4) | async-done | bytes 196640 | tf_op jit(solution)/shard_map/all_to_all | solution.py:46
  238.0 7.7 %all-to-all-start.8 = ((bf16[64,12,128]{2,1,0:T(8,128)(2,1)}), bf16[64,12,128]{2,1,0:T(8,128)(2,1)}, u32[]{:S(2)}, u32[]{:S(2)}) async-start(bf16[64,12,128]{2,1,0:T(8,128)(2,1)} %reshape.121), calls=%async_computation.8 | async-start | bytes 524288 | tf_op jit(solution)/shard_map/all_to_all | solution.py:46
  253.6 4.8 %all-to-all-done.8 = bf16[64,12,128]{2,1,0:T(8,128)(2,1)} async-done(((bf16[64,12,128]{2,1,0:T(8,128)(2,1)}), bf16[64,12,128]{2,1,0:T(8,128)(2,1)}, u32[]{:S(2)}, u32[]{:S(2)}) %all-to-all-start.8) | async-done | bytes 196640 | tf_op jit(solution)/shard_map/all_to_all | solution.py:46
  258.4 8.1 %all-to-all-start.6 = ((bf16[64,12,128]{2,1,0:T(8,128)(2,1)}), bf16[64,12,128]{2,1,0:T(8,128)(2,1)}, u32[]{:S(2)}, u32[]{:S(2)}) async-start(bf16[64,12,128]{2,1,0:T(8,128)(2,1)} %reshape.119), calls=%async_computation.6 | async-start | bytes 524288 | tf_op jit(solution)/shard_map/all_to_all | solution.py:46
  267.7 11.5 %all-to-all-done.6 = bf16[64,12,128]{2,1,0:T(8,128)(2,1)} async-done(((bf16[64,12,128]{2,1,0:T(8,128)(2,1)}), bf16[64,12,128]{2,1,0:T(8,128)(2,1)}, u32[]{:S(2)}, u32[]{:S(2)}) %all-to-all-start.6) | async-done | bytes 196640 | tf_op jit(solution)/shard_map/all_to_all | solution.py:46
  279.9 6.2 %all-to-all-start.11 = ((bf16[64,2,768]{2,1,0:T(2,128)(2,1)}), bf16[64,2,768]{2,1,0:T(2,128)(2,1)}, u32[]{:S(2)}, u32[]{:S(2)}) async-start(bf16[64,2,768]{2,1,0:T(2,128)(2,1)} %broadcast_in_dim.17), calls=%async_computation.11 | async-start | bytes 393216 | tf_op jit(solution)/shard_map/all_to_all | solution.py:15
  286.2 12.2 %all-to-all-done.11 = bf16[64,2,768]{2,1,0:T(2,128)(2,1)} async-done(((bf16[64,2,768]{2,1,0:T(2,128)(2,1)}), bf16[64,2,768]{2,1,0:T(2,128)(2,1)}, u32[]{:S(2)}, u32[]{:S(2)}) %all-to-all-start.11) | async-done | bytes 196640 | tf_op jit(solution)/shard_map/all_to_all | solution.py:15
  299.2 5.7 %all-to-all-start.5 = ((bf16[64,12,128]{2,1,0:T(8,128)(2,1)}), bf16[64,12,128]{2,1,0:T(8,128)(2,1)S(1)}, u32[]{:S(2)}, u32[]{:S(2)}) async-start(bf16[64,12,128]{2,1,0:T(8,128)(2,1)} %broadcast_in_dim.14), calls=%async_computation.5 | async-start | bytes 524288 | tf_op jit(solution)/shard_map/all_to_all | solution.py:15
  305.9 12.0 %all-to-all-done.5 = bf16[64,12,128]{2,1,0:T(8,128)(2,1)S(1)} async-done(((bf16[64,12,128]{2,1,0:T(8,128)(2,1)}), bf16[64,12,128]{2,1,0:T(8,128)(2,1)S(1)}, u32[]{:S(2)}, u32[]{:S(2)}) %all-to-all-start.5) | async-done | bytes 196640 | tf_op jit(solution)/shard_map/all_to_all | solution.py:15
  318.7 6.1 %all-to-all-start.9 = ((bf16[64,12,128]{2,1,0:T(8,128)(2,1)}), bf16[64,12,128]{2,1,0:T(8,128)(2,1)}, u32[]{:S(2)}, u32[]{:S(2)}) async-start(bf16[64,12,128]{2,1,0:T(8,128)(2,1)} %broadcast_in_dim.16), calls=%async_computation.9 | async-start | bytes 524288 | tf_op jit(solution)/shard_map/all_to_all | solution.py:15
  325.8 11.9 %all-to-all-done.9 = bf16[64,12,128]{2,1,0:T(8,128)(2,1)} async-done(((bf16[64,12,128]{2,1,0:T(8,128)(2,1)}), bf16[64,12,128]{2,1,0:T(8,128)(2,1)}, u32[]{:S(2)}, u32[]{:S(2)}) %all-to-all-start.9) | async-done | bytes 196640 | tf_op jit(solution)/shard_map/all_to_all | solution.py:15
  338.5 6.1 %all-to-all-start.7 = ((bf16[64,12,128]{2,1,0:T(8,128)(2,1)}), bf16[64,12,128]{2,1,0:T(8,128)(2,1)}, u32[]{:S(2)}, u32[]{:S(2)}) async-start(bf16[64,12,128]{2,1,0:T(8,128)(2,1)} %broadcast_in_dim.15), calls=%async_computation.7 | async-start | bytes 524288 | tf_op jit(solution)/shard_map/all_to_all | solution.py:15
  348.2 4.4 %copy.60 = bf16[12,512,128]{2,0,1:T(8,128)(2,1)} copy(bf16[12,512,128]{1,2,0:T(8,128)(2,1)} %pad_maximum_fusion) | data formatting | bytes 3145728 | tf_op jit(solution)/shard_map/concatenate | solution.py:70
  352.7 4.9 %all-to-all-done.7 = bf16[64,12,128]{2,1,0:T(8,128)(2,1)} async-done(((bf16[64,12,128]{2,1,0:T(8,128)(2,1)}), bf16[64,12,128]{2,1,0:T(8,128)(2,1)}, u32[]{:S(2)}, u32[]{:S(2)}) %all-to-all-start.7) | async-done | bytes 196640 | tf_op jit(solution)/shard_map/all_to_all | solution.py:15
  357.6 4.5 %all-to-all-start.1 = ((bf16[12,512,128]{2,0,1:T(8,128)(2,1)}), bf16[12,512,128]{2,0,1:T(8,128)(2,1)}, u32[]{:S(2)}, u32[]{:S(2)}) async-start(bf16[12,512,128]{2,0,1:T(8,128)(2,1)} %copy.60), calls=%async_computation.1 | async-start | bytes 4194304 | tf_op jit(solution)/shard_map/all_to_all | solution.py:71
  (111 shorter events, 107.2 us)
Async XLA Ops:
  7.2 1.9 copy-start
  7.2 184.3 %all-gather.2.cloned.1.call-start = ((), (), s32[]{:S(2)}) async-start(), calls=%async_computation.12 | async-start | bytes 2129920 | tf_op jit(solution)/shard_map/all_gather | solution.py:65
  11.8 6.7 %copy-start.12 = (bf16[768,128]{1,0:T(8,128)(2,1)S(1)}, bf16[768,128]{1,0:T(8,128)(2,1)}, u32[]{:S(2)}) copy-start(bf16[768,128]{1,0:T(8,128)(2,1)} %param.8) | copy-start | bytes 589828
  20.3 6.7 %copy-start.11 = (bf16[768,128]{1,0:T(8,128)(2,1)S(1)}, bf16[768,128]{1,0:T(8,128)(2,1)}, u32[]{:S(2)}) copy-start(bf16[768,128]{1,0:T(8,128)(2,1)} %param.9) | copy-start | bytes 589828
  28.8 6.7 %copy-start.16 = (bf16[128,768]{1,0:T(8,128)(2,1)S(1)}, bf16[128,768]{1,0:T(8,128)(2,1)}, u32[]{:S(2)}) copy-start(bf16[128,768]{1,0:T(8,128)(2,1)} %param.11) | copy-start | bytes 589828
  45.9 1.8 copy-start.14
  45.9 1.8 copy-start.15
  116.4 1.3 copy-start.10
  136.0 59.4 %all-to-all-start.3 = ((bf16[2,2,2304,128]{3,2,1,0:T(8,128)(2,1)}), bf16[2,2,2304,128]{3,2,1,0:T(8,128)(2,1)}, u32[]{:S(2)}, u32[]{:S(2)}) async-start(bf16[2,2,2304,128]{3,2,1,0:T(8,128)(2,1)} %broadcast_in_dim.13), calls=%async_computation.3 | async-start | bytes 4718592 | tf_op jit(solution)/shard_map/all_to_all | solution.py:15
  191.5 2.5 copy-start.1
  195.4 22.2 %all-to-all-start.10 = ((bf16[64,2,768]{2,1,0:T(2,128)(2,1)}), bf16[64,2,768]{2,1,0:T(2,128)(2,1)S(1)}, u32[]{:S(2)}, u32[]{:S(2)}) async-start(bf16[64,2,768]{2,1,0:T(2,128)(2,1)} %reshape.123), calls=%async_computation.10 | async-start | bytes 393216 | tf_op jit(solution)/shard_map/all_to_all | solution.py:46
  218.3 19.7 %all-to-all-start.4 = ((bf16[64,12,128]{2,1,0:T(8,128)(2,1)}), bf16[64,12,128]{2,1,0:T(8,128)(2,1)S(1)}, u32[]{:S(2)}, u32[]{:S(2)}) async-start(bf16[64,12,128]{2,1,0:T(8,128)(2,1)} %reshape.117), calls=%async_computation.4 | async-start | bytes 524288 | tf_op jit(solution)/shard_map/all_to_all | solution.py:46
  238.0 20.3 %all-to-all-start.8 = ((bf16[64,12,128]{2,1,0:T(8,128)(2,1)}), bf16[64,12,128]{2,1,0:T(8,128)(2,1)}, u32[]{:S(2)}, u32[]{:S(2)}) async-start(bf16[64,12,128]{2,1,0:T(8,128)(2,1)} %reshape.121), calls=%async_computation.8 | async-start | bytes 524288 | tf_op jit(solution)/shard_map/all_to_all | solution.py:46
  258.4 20.8 %all-to-all-start.6 = ((bf16[64,12,128]{2,1,0:T(8,128)(2,1)}), bf16[64,12,128]{2,1,0:T(8,128)(2,1)}, u32[]{:S(2)}, u32[]{:S(2)}) async-start(bf16[64,12,128]{2,1,0:T(8,128)(2,1)} %reshape.119), calls=%async_computation.6 | async-start | bytes 524288 | tf_op jit(solution)/shard_map/all_to_all | solution.py:46
  279.9 18.5 %all-to-all-start.11 = ((bf16[64,2,768]{2,1,0:T(2,128)(2,1)}), bf16[64,2,768]{2,1,0:T(2,128)(2,1)}, u32[]{:S(2)}, u32[]{:S(2)}) async-start(bf16[64,2,768]{2,1,0:T(2,128)(2,1)} %broadcast_in_dim.17), calls=%async_computation.11 | async-start | bytes 393216 | tf_op jit(solution)/shard_map/all_to_all | solution.py:15
  299.2 18.7 %all-to-all-start.5 = ((bf16[64,12,128]{2,1,0:T(8,128)(2,1)}), bf16[64,12,128]{2,1,0:T(8,128)(2,1)S(1)}, u32[]{:S(2)}, u32[]{:S(2)}) async-start(bf16[64,12,128]{2,1,0:T(8,128)(2,1)} %broadcast_in_dim.14), calls=%async_computation.5 | async-start | bytes 524288 | tf_op jit(solution)/shard_map/all_to_all | solution.py:15
  317.9 29.0 %copy-start.9 = (bf16[64,12,128]{2,1,0:T(8,128)(2,1)}, bf16[64,12,128]{2,1,0:T(8,128)(2,1)S(1)}, u32[]{:S(2)}) copy-start(bf16[64,12,128]{2,1,0:T(8,128)(2,1)S(1)} %all-to-all-done.5) | copy-start | bytes 589828
  318.7 19.1 %all-to-all-start.9 = ((bf16[64,12,128]{2,1,0:T(8,128)(2,1)}), bf16[64,12,128]{2,1,0:T(8,128)(2,1)}, u32[]{:S(2)}, u32[]{:S(2)}) async-start(bf16[64,12,128]{2,1,0:T(8,128)(2,1)} %broadcast_in_dim.16), calls=%async_computation.9 | async-start | bytes 524288 | tf_op jit(solution)/shard_map/all_to_all | solution.py:15
  338.5 19.1 %all-to-all-start.7 = ((bf16[64,12,128]{2,1,0:T(8,128)(2,1)}), bf16[64,12,128]{2,1,0:T(8,128)(2,1)}, u32[]{:S(2)}, u32[]{:S(2)}) async-start(bf16[64,12,128]{2,1,0:T(8,128)(2,1)} %broadcast_in_dim.15), calls=%async_computation.7 | async-start | bytes 524288 | tf_op jit(solution)/shard_map/all_to_all | solution.py:15
  344.6 2.3 copy-start.8
  357.6 30.2 %all-to-all-start.1 = ((bf16[12,512,128]{2,0,1:T(8,128)(2,1)}), bf16[12,512,128]{2,0,1:T(8,128)(2,1)}, u32[]{:S(2)}, u32[]{:S(2)}) async-start(bf16[12,512,128]{2,0,1:T(8,128)(2,1)} %copy.60), calls=%async_computation.1 | async-start | bytes 4194304 | tf_op jit(solution)/shard_map/all_to_all | solution.py:71
  390.6 1.1 copy-start.3
  391.3 1.2 copy-start.4
  392.3 1.2 copy-start.2
  (4 other events, 3.1 us)
Sparse Core Ops, SparseCore 0:
  117.7 73.7 all-gather.1
where the time goes:
time: 405 us; the launch traced here: 402 us
  waiting for transfers between devices  122 us (30%)
  blocking collectives  83.4 us (21%)
  local copies, waits for them, and re-layouts  76 us (19%)
  starting transfers between devices  65.9 us (16%)
  matrix products  26.7 us (7%)
  between operations  14.4 us (4%)
  other arithmetic  13.6 us (3%)
    all_to_all x1, blocking collectives, sum_at_owner(): lax.all_to_all(in_blocks(value, dim, count), axis, 0, 0, tiled=True)  67.9 us
    all_gather x1, waiting for transfers between devices, side_by_side(): lax.all_gather(both, axis, axis=dim, tiled=True)  50.6 us
    all_to_all x5, waiting for transfers between devices, from_everyone(): lax.all_to_all(jnp.broadcast_to(value[None], (count, *value.shape)), axis...  41.1 us
    all_to_all x4, starting transfers between devices, sum_at_owner(): lax.all_to_all(in_blocks(value, dim, count), axis, 0, 0, tiled=True)  32.4 us
    all_to_all x5, starting transfers between devices, from_everyone(): lax.all_to_all(jnp.broadcast_to(value[None], (count, *value.shape)), axis...  29 us
    all_to_all x4, waiting for transfers between devices, sum_at_owner(): lax.all_to_all(in_blocks(value, dim, count), axis, 0, 0, tiled=True)  27.5 us
    all_to_all x1, blocking collectives, from_everyone(): lax.all_to_all(jnp.broadcast_to(value[None], (count, *value.shape)), axis...  15.6 us
    split x4, local copies, waits for them, and re-layouts, in_one_piece(): jnp.split(whole, [sum(widths[:k]) for k in range(1, len(widths))], axis=a...  8.35 us
  transfers between devices with their start and end apart: 11, of which 10 were waited for; matrix products, arithmetic and copies ran while one was open for 15% of the time, Pallas kernels for 0%

commit v1 on v0

v1 whole, which is shorter than its diff:
```python
import math

import jax
import jax.numpy as jnp
from jax import lax
from jax.experimental import pallas as pl
from jax.experimental.pallas import tpu as pltpu
from jax.sharding import Mesh
from jax.sharding import PartitionSpec as P

AXES = ("y", "zh", "x", "zl", "core")
SEQ = ("y", "zh", "x")
HEAD = ("zl", "core")
ROWS, COLS, D, HEAD_DIM, HEADS = 4, 512, 768, 64, 2
WIDTH = HEADS * HEAD_DIM
ALL_ROWS = 256
C = 1.0 / (math.sqrt(HEAD_DIM) * math.sqrt(ALL_ROWS))
INV_ROOT = 1.0 / math.sqrt(ALL_ROWS * COLS)
COPIES = 128
F32, BF16 = jnp.float32, jnp.bfloat16


def nt(a, b):
    return lax.dot_general(a, b, (((1,), (1,)), ((), ())), preferred_element_type=F32)


def nn(a, b):
    return lax.dot_general(a, b, (((1,), (0,)), ((), ())), preferred_element_type=F32)


def tn(a, b):
    return lax.dot_general(a, b, (((0,), (0,)), ((), ())), preferred_element_type=F32)


class Copies:
    def __init__(self, send_sem, recv_sem):
        self.send_sem, self.recv_sem, self.made = send_sem, recv_sem, []

    def send(self, src, dst, device):
        k = len(self.made)
        copy = pltpu.make_async_remote_copy(
            src_ref=src,
            dst_ref=dst,
            send_sem=self.send_sem.at[k],
            recv_sem=self.recv_sem.at[k],
            device_id=device,
            device_id_type=pl.DeviceIdType.MESH,
        )
        copy.start()
        self.made.append(copy)
        return copy

    def drain(self):
        for copy in self.made:
            copy.wait_send()


class RingSum:
    def __init__(self, copies, piece, rel, rcv, tmp, right, left):
        self.copies, self.piece, self.rel, self.rcv, self.tmp = copies, piece, rel, rcv, tmp
        self.right, self.left = right, left

    def start(self):
        send, piece = self.copies.send, self.piece
        self.c1 = send(piece(2, 0), self.rel.at[0], self.right)
        self.c2 = send(piece(2, 1), self.rel.at[1], self.left)
        self.c3 = send(piece(1, 1), self.rcv.at[0, 1], self.right)
        self.c4 = send(piece(3, 0), self.rcv.at[1, 0], self.left)

    def relay(self):
        send, piece = self.copies.send, self.piece
        self.c1.wait_recv()
        self.tmp[0] = (piece(1, 0)[...].astype(F32) + self.rel[0].astype(F32)).astype(BF16)
        self.c2.wait_recv()
        self.tmp[1] = (piece(3, 1)[...].astype(F32) + self.rel[1].astype(F32)).astype(BF16)
        self.c5 = send(self.tmp.at[0], self.rcv.at[0, 0], self.right)
        self.c6 = send(self.tmp.at[1], self.rcv.at[1, 1], self.left)

    def finish(self):
        for copy in (self.c3, self.c4, self.c5, self.c6):
            copy.wait_recv()
        return [
            self.piece(0, half)[...].astype(F32)
            + self.rcv[0, half].astype(F32)
            + self.rcv[1, half].astype(F32)
            for half in range(2)
        ]


class RingGather:
    def __init__(self, copies, block, right, left):
        self.copies, self.block, self.right, self.left = copies, block, right, left

    def start(self):
        whole = self.block(0, None)
        self.d1 = self.copies.send(whole, whole, self.right)
        self.d2 = self.copies.send(whole, whole, self.left)

    def relay(self):
        self.d1.wait_recv()
        far = self.block(3, 0)
        self.e1 = self.copies.send(far, far, self.right)
        self.d2.wait_recv()
        far = self.block(1, 1)
        self.e2 = self.copies.send(far, far, self.left)

    def finish(self):
        self.e1.wait_recv()
        self.e2.wait_recv()


def kernel(
    x_hbm, g_hbm, wq_hbm, wk_hbm, wv_hbm, wo_hbm,
    gin_ref, wt_ref,
    xv, gv, wo, wfull, wt, proj, part,
    rel1, rcv1, tmp1, sum1, rel2, rcv2, tmp2, sum2, rcv3,
    pd, att, grad, gall,
    wacc, wpart, wrel1, wrcv1, wtmp1, wsum1, wrel2, wrcv2, wtmp2, wrcv3, wfin,
    load_sem, send_sem, recv_sem,
):
    y, zh, x, zl, co = (lax.axis_index(n) for n in AXES)
    a = x * (1 - co) + y * co
    b = y * (1 - co) + x * co
    head = zl * 2 + co

    def dev(da=0, db=0, dc=0, dzl=0, dco=0):
        return (
            lax.rem(y + da * co + db * (1 - co), 4),
            lax.rem(zh + dc, 4),
            lax.rem(x + da * (1 - co) + db * co, 4),
            lax.rem(zl + dzl, 2),
            lax.rem(co + dco, 2),
        )

    a_right, a_left = dev(da=1), dev(da=3)
    b_right, b_left = dev(db=1), dev(db=3)
    z_others = [dev(dc=k) for k in (1, 2, 3)]
    h_core, h_chip, h_both = dev(dco=1), dev(dzl=1), dev(dzl=1, dco=1)

    def at_a(off, size):
        return pl.ds(pl.multiple_of(lax.rem(a + off, 4) * size, size), size)

    mine = pl.ds(pl.multiple_of(head * WIDTH, WIDTH), WIDTH)
    loads = [
        pltpu.make_async_copy(w.at[...], wfull.at[t, :, mine], load_sem.at[t])
        for t, w in enumerate((wq_hbm, wk_hbm, wv_hbm))
    ]
    loads.append(pltpu.make_async_copy(x_hbm, xv, load_sem.at[3]))
    loads.append(pltpu.make_async_copy(wo_hbm, wo, load_sem.at[4]))
    loads.append(pltpu.make_async_copy(g_hbm, gv, load_sem.at[5]))
    for load in loads:
        load.start()

    barrier = pltpu.get_barrier_semaphore()
    friends = [a_right, a_left, b_right, b_left, *z_others, h_core, h_chip, h_both]
    for friend in friends:
        pl.semaphore_signal(barrier, inc=1, device_id=friend, device_id_type=pl.DeviceIdType.MESH)

    copies = Copies(send_sem, recv_sem)
    for load in loads[:4]:
        load.wait()
    for t in range(3):
        wt[t * WIDTH : (t + 1) * WIDTH, :] = wfull[t, :, mine].T

    def project(r, _):
        res = nt(wt[...], xv[r]).astype(BF16)
        at = pl.ds(pl.multiple_of(r * HEAD_DIM, HEAD_DIM), HEAD_DIM)
        for t in range(3):
            for h in range(HEADS):
                k = t * WIDTH + h * HEAD_DIM
                proj[t, h, at, :] = res[k : k + HEAD_DIM]
        return 0

    lax.fori_loop(0, ROWS, project, 0)

    def products(m, left, right):
        def one(k, _):
            h, blk = k // 4, lax.rem(k, 4)
            at = pl.ds(pl.multiple_of(blk * 128, 128), 128)
            part[m, h, at, :] = tn(proj[left, h, :, at], proj[right, h]).astype(BF16)
            return 0

        lax.fori_loop(0, 4 * HEADS, one, 0)

    products(0, 0, 1)
    pl.semaphore_wait(barrier, len(friends))

    def ring1(m):
        return RingSum(
            copies,
            lambda off, half: part.at[m, half, at_a(off, 128), :],
            rel1.at[m], rcv1.at[m], tmp1.at[m], a_right, a_left,
        )

    first = [ring1(0), ring1(1)]
    first[0].start()
    to_core = [copies.send(wfull.at[t, :, mine], wfull.at[t, :, mine], h_core) for t in range(3)]
    to_chip = [copies.send(wfull.at[t, :, mine], wfull.at[t, :, mine], h_chip) for t in range(3)]

    for load in loads[4:]:
        load.wait()

    def project_grad(r, _):
        res = nt(wo[...], gv[r]).astype(BF16)
        at = pl.ds(pl.multiple_of(r * HEAD_DIM, HEAD_DIM), HEAD_DIM)
        for h in range(HEADS):
            proj[3, h, at, :] = res[h * HEAD_DIM : (h + 1) * HEAD_DIM]
        return 0

    lax.fori_loop(0, ROWS, project_grad, 0)
    products(1, 3, 2)
    first[1].start()

    def at_b(off, size):
        return pl.ds(pl.multiple_of(lax.rem(b + off, 4) * size, size), size)

    def ring2(m):
        return RingSum(
            copies,
            lambda off, half: sum1.at[m, half, at_b(off, 32), :],
            rel2.at[m], rcv2.at[m], tmp2.at[m], b_right, b_left,
        )

    second = [ring2(0), ring2(1)]
    first[0].relay()
    first[1].relay()
    for m in range(2):
        for half, total in enumerate(first[m].finish()):
            sum1[m, half] = total.astype(BF16)
        second[m].start()
    second[0].relay()
    second[1].relay()

    other = lax.rem(zl + 1, 2) * 2 + co
    theirs = pl.ds(pl.multiple_of(other * WIDTH, WIDTH), WIDTH)
    forward = []
    for t in range(3):
        to_chip[t].wait_recv()
        forward.append(copies.send(wfull.at[t, :, theirs], wfull.at[t, :, theirs], h_core))

    def spot(off):
        place = lax.rem(zh + off, 4)
        return place // 2, pl.ds(pl.multiple_of(lax.rem(place, 2) * 16, 16), 16)

    third = []
    for m in range(2):
        for half, total in enumerate(second[m].finish()):
            sum2[m, half] = total.astype(BF16)
        third.append([])
        for k in range(3):
            h, at = spot(k + 1)
            third[m].append(copies.send(sum2.at[m, h, at, :], rcv3.at[m, k], z_others[k]))

    totals = []
    for m in range(2):
        h, at = spot(0)
        total = sum2[m, h, at, :].astype(F32)
        for k in range(3):
            third[m][k].wait_recv()
            total = total + rcv3[m, k].astype(F32)
        totals.append(total)

    exponent = jnp.exp(C * totals[0])
    probs = exponent / jnp.sum(exponent, axis=1, keepdims=True)
    inner = jnp.sum(probs * totals[1], axis=1, keepdims=True)
    dlog = C * probs * (totals[1] - inner)
    own_h, _ = spot(0)
    row = a * 128 + b * 32 + lax.rem(zh, 2) * 16
    own_rows = pl.ds(pl.multiple_of(row, 16), 16)
    pd[0, own_h, own_rows, :] = probs.astype(BF16)
    pd[1, own_h, own_rows, :] = dlog.astype(BF16)
    own = pd.at[:, own_h, own_rows, :]
    spread = [copies.send(own, own, z_others[k]) for k in range(3)]
    for copy in spread:
        copy.wait_recv()

    def block_b(off, half):
        row = a * 128 + lax.rem(b + off, 4) * 32
        at = pl.ds(pl.multiple_of(row, 32), 32)
        return pd.at[:, :, at, :] if half is None else pd.at[:, half, at, :]

    gather_b = RingGather(copies, block_b, b_right, b_left)
    gather_b.start()
    gather_b.relay()
    gather_b.finish()

    def block_a(m):
        def block(off, half):
            at = at_a(off, 128)
            return pd.at[m, :, at, :] if half is None else pd.at[m, half, at, :]

        return block

    gather_a = [RingGather(copies, block_a(m), a_right, a_left) for m in range(2)]
    gather_a[0].start()
    gather_a[1].start()
    gather_a[0].relay()
    gather_a[0].finish()

    def pair_value(h, _):
        p = pd[0, h]
        att[h] = nt(proj[2, h], p).astype(BF16).reshape(ROWS, HEAD_DIM, COLS)
        grad[2, h] = nn(proj[3, h], p).astype(BF16).reshape(ROWS, HEAD_DIM, COLS)
        return 0

    lax.fori_loop(0, HEADS, pair_value, 0)
    gather_a[1].relay()

    def to_heads(t):
        sent = []
        for device, dzl, dco in ((h_chip, 1, 0), (h_both, 1, 1), (h_core, 0, 1)):
            h = lax.rem(zl + dzl, 2) * 2 + lax.rem(co + dco, 2)
            at = pl.ds(pl.multiple_of(h * 128, 128), 128)
            sent.append(copies.send(grad.at[t, :, :, :, at], gall.at[t, head], device))
        keep = pltpu.make_async_copy(grad.at[t, :, :, :, mine], gall.at[t, head], load_sem.at[6 + t])
        keep.start()
        return sent, keep

    moved = {2: to_heads(2)}

    def weight_part(p, kinds):
        def one(r, _):
            for k, (source, t) in enumerate(kinds):
                src = att if t is None else grad.at[t]
                lhs = jnp.concatenate([src[0, r], src[1, r]], axis=0)
                at = slice(k * WIDTH, (k + 1) * WIDTH)
                wacc[at, :] = jnp.where(r == 0, 0.0, wacc[at, :]) + nn(lhs, source[r])
            return 0

        lax.fori_loop(0, ROWS, one, 0)
        wpart[p] = wacc[...].astype(BF16)

    def halves(half):
        return slice(half * 384, (half + 1) * 384)

    def wring1(p):
        return RingSum(
            copies,
            lambda off, half: wpart.at[p, at_a(off, 64), halves(half)],
            wrel1.at[p], wrcv1.at[p], wtmp1.at[p], a_right, a_left,
        )

    def wring2(p):
        return RingSum(
            copies,
            lambda off, half: wsum1.at[p, at_b(off, 16), halves(half)],
            wrel2.at[p], wrcv2.at[p], wtmp2.at[p], b_right, b_left,
        )

    wfirst = [wring1(0), wring1(1)]
    wsecond = [wring2(0), wring2(1)]
    weight_part(0, ((xv, 2), (gv, None)))
    wfirst[0].start()
    gather_a[1].finish()

    def pair_score(h, _):
        d = pd[1, h]
        grad[0, h] = nt(proj[1, h], d).astype(BF16).reshape(ROWS, HEAD_DIM, COLS)
        grad[1, h] = nn(proj[0, h], d).astype(BF16).reshape(ROWS, HEAD_DIM, COLS)
        return 0

    lax.fori_loop(0, HEADS, pair_score, 0)
    moved[0] = to_heads(0)
    moved[1] = to_heads(1)
    wfirst[0].relay()
    weight_part(1, ((xv, 0), (xv, 1)))
    wfirst[1].start()

    def end_first(p):
        for half, total in enumerate(wfirst[p].finish()):
            wsum1[p, :, halves(half)] = total.astype(BF16)
        wsecond[p].start()

    wthird = []

    def end_second(p):
        for half, total in enumerate(wsecond[p].finish()):
            wrcv3[p, zh, :, halves(half)] = total.astype(BF16)
        own = wrcv3.at[p, zh]
        wthird.append([copies.send(own, own, device) for device in z_others])

    wgather_b, wgather_a = [], []

    def end_third(p):
        for copy in wthird[p]:
            copy.wait_recv()
        total = wrcv3[p, 0].astype(F32) + wrcv3[p, 1].astype(F32)
        total = total + wrcv3[p, 2].astype(F32) + wrcv3[p, 3].astype(F32)
        wfin[p, pl.ds(pl.multiple_of(a * 64 + b * 16, 16), 16), :] = total.astype(BF16)

        def block_b(off, half):
            at = pl.ds(pl.multiple_of(a * 64 + lax.rem(b + off, 4) * 16, 16), 16)
            return wfin.at[p, at, :] if half is None else wfin.at[p, at, halves(half)]

        def block_a(off, half):
            at = at_a(off, 64)
            return wfin.at[p, at, :] if half is None else wfin.at[p, at, halves(half)]

        wgather_b.append(RingGather(copies, block_b, b_right, b_left))
        wgather_a.append(RingGather(copies, block_a, a_right, a_left))
        wgather_b[p].start()

    end_first(0)
    wsecond[0].relay()
    wfirst[1].relay()
    end_second(0)
    end_first(1)
    wsecond[1].relay()
    end_third(0)
    end_second(1)
    wgather_b[0].relay()
    wgather_b[0].finish()
    wgather_a[0].start()
    end_third(1)
    wgather_a[0].relay()
    wgather_b[1].relay()
    wgather_b[1].finish()
    wgather_a[1].start()
    wgather_a[1].relay()

    for copy in to_core + forward:
        copy.wait_recv()
    for t in range(3):
        sent, keep = moved[t]
        keep.wait()
        for copy in sent:
            copy.wait_recv()

    def block_inputs(k, _):
        r = k * 2
        total = None
        for t in range(3):
            sides = [
                jnp.concatenate([gall[t, hd, h, r + s] for hd in range(4) for h in range(HEADS)], axis=0)
                for s in range(2)
            ]
            term = nn(wfull[t], jnp.concatenate(sides, axis=1))
            total = term if total is None else total + term
        flat = total.T.astype(BF16)
        gin_ref[r] = flat[:128]
        gin_ref[r + 1] = flat[128:]
        return 0

    lax.fori_loop(0, 2, block_inputs, 0)
    wgather_a[0].finish()
    wgather_a[1].finish()
    wt_ref[...] = wfin[...]
    copies.drain()


def body(inputs, out_grad, w_query, w_key, w_value, w_output):
    vmem = lambda *shape: pltpu.VMEM(shape, BF16)
    gin, wts = pl.pallas_call(
        kernel,
        out_shape=(
            jax.ShapeDtypeStruct((ROWS, 128, D), BF16),
            jax.ShapeDtypeStruct((2, 2 * WIDTH, D), BF16),
        ),
        in_specs=[pl.BlockSpec(memory_space=pl.ANY)] * 6,
        out_specs=(pl.BlockSpec(memory_space=pltpu.VMEM),) * 2,
        scratch_shapes=[
            vmem(ROWS, COLS, D),
            vmem(ROWS, COLS, D),
            vmem(WIDTH, D),
            vmem(3, D, 4 * WIDTH),
            vmem(3 * WIDTH, D),
            vmem(4, HEADS, ROWS * HEAD_DIM, COLS),
            vmem(2, HEADS, COLS, COLS),
            vmem(2, 2, 128, COLS),
            vmem(2, 2, 2, 128, COLS),
            vmem(2, 2, 128, COLS),
            vmem(2, HEADS, 128, COLS),
            vmem(2, 2, 32, COLS),
            vmem(2, 2, 2, 32, COLS),
            vmem(2, 2, 32, COLS),
            vmem(2, HEADS, 32, COLS),
            vmem(2, 3, 16, COLS),
            vmem(2, HEADS, COLS, COLS),
            vmem(HEADS, ROWS, HEAD_DIM, COLS),
            vmem(3, HEADS, ROWS, HEAD_DIM, COLS),
            vmem(3, 4, HEADS, ROWS, HEAD_DIM, 128),
            pltpu.VMEM((2 * WIDTH, D), F32),
            vmem(2, 2 * WIDTH, D),
            vmem(2, 2, 64, 384),
            vmem(2, 2, 2, 64, 384),
            vmem(2, 2, 64, 384),
            vmem(2, 64, D),
            vmem(2, 2, 16, 384),
            vmem(2, 2, 2, 16, 384),
            vmem(2, 2, 16, 384),
            vmem(2, 4, 16, D),
            vmem(2, 2 * WIDTH, D),
            pltpu.SemaphoreType.DMA((9,)),
            pltpu.SemaphoreType.DMA((COPIES,)),
            pltpu.SemaphoreType.DMA((COPIES,)),
        ],
        compiler_params=pltpu.CompilerParams(
            collective_id=0, has_side_effects=True, vmem_limit_bytes=56 * 1024 * 1024
        ),
        name="tied_row_attention_grad",
    )(inputs, out_grad, w_query, w_key, w_value, w_output)
    scaled = wts.astype(F32) * INV_ROOT
    turned = lambda w: w.T
    return (
        gin,
        turned(scaled[1, :WIDTH]),
        turned(scaled[1, WIDTH:]),
        turned(scaled[0, :WIDTH]),
        scaled[0, WIDTH:],
    )


def solution(mesh):
    finer = Mesh(mesh.devices.reshape(4, 4, 4, 2, 2), AXES)
    return jax.shard_map(
        body,
        mesh=finer,
        in_specs=(
            P(SEQ, None, None),
            P(SEQ, None, None),
            P(None, HEAD),
            P(None, HEAD),
            P(None, HEAD),
            P(HEAD, None),
        ),
        out_specs=(
            P(SEQ, HEAD, None),
            P(None, HEAD),
            P(None, HEAD),
            P(None, HEAD),
            P(HEAD, None),
        ),
        check_vma=False,
    )
```

time: 405 us -> 117 us (0.29)
  waiting for transfers between devices: 122 us -> 0 us
  Pallas kernels: 0 us -> 111 us
  blocking collectives: 83.4 us -> 0 us
  local copies, waits for them, and re-layouts: 76 us -> 4.52 us
  starting transfers between devices: 65.9 us -> 0 us
  matrix products: 26.7 us -> 0 us
  between operations: 14.4 us -> 0.65 us
  other arithmetic: 13.6 us -> 1.26 us
    pallas_call x0 -> x1, Pallas kernels: none -> 111 us  [body(): pl.pallas_call(kernel, out_shape=(jax.ShapeDtypeStruct((ROWS, 128, D), BF...]
    all_to_all x2 -> x0, blocking collectives: 83.4 us -> none  [the longest x1 67.9 us: sum_at_owner(): lax.all_to_all(in_blocks(value, dim, count), axis, 0, 0, tiled=True)]
    all_to_all x10 -> x0, waiting for transfers between devices: 71.1 us -> none  [the longest x5 41.1 us: from_everyone(): lax.all_to_all(jnp.broadcast_to(value[None], (count, *value.shape)), axis...]
    all_to_all x10 -> x0, starting transfers between devices: 65.9 us -> none  [the longest x4 32.4 us: sum_at_owner(): lax.all_to_all(in_blocks(value, dim, count), axis, 0, 0, tiled=True)]
    all_gather x1 -> x0, waiting for transfers between devices: 50.6 us -> none  [side_by_side(): lax.all_gather(both, axis, axis=dim, tiled=True)]
    reshape x12 -> x0, local copies, waits for them, and re-layouts: 31.7 us -> none  [the longest x2 6.74 us: body(): value_four = value_proj.reshape(shape_heads)]
    dot_general x17 -> x0, matrix products: 26.7 us -> none  [the longest x4 6.27 us: times_transpose(): lax.dot_general(left, right, (((1,), (1,)), ((), ())), preferred_element_...]
    split x5 -> x0, local copies, waits for them, and re-layouts: 9 us -> none  [the longest x4 8.35 us: in_one_piece(): jnp.split(whole, [sum(widths[:k]) for k in range(1, len(widths))], axis=a...]
  transfers between devices with their start and end apart: 11 -> 0, of which waited for: 10 -> 0; matrix products, arithmetic and copies ran while one was open for 15% -> 0% of each run, Pallas kernels for 0% -> 0%
where the time goes in v1:
time: 117 us
  Pallas kernels  111 us (95%)
  local copies, waits for them, and re-layouts  4.52 us (4%)
  other arithmetic  1.26 us (1%)
    pallas_call x1, Pallas kernels, body(): pl.pallas_call(kernel, out_shape=(jax.ShapeDtypeStruct((ROWS, 128, D), BF...  111 us
    unnamed x6, local copies, waits for them, and re-layouts  3.62 us

profile of v1, /device:TPU:2, one launch (start us, length us, event | category | flops | bytes accessed | tf_op | source)
XLA Modules:
  0.0 117.2 jit_solution(893745862603443883)
XLA Ops:
  0.6 110.7 %tied_row_attention_grad.1 = (bf16[4,128,768]{2,1,0:T(8,128)(2,1)}, bf16[2,256,768]{2,1,0:T(8,128)(2,1)}) custom-call(bf16[4,512,768]{2,1,0:T(8,128)(2,1)} %x_hbm.1, bf16[4,512,768]{2,1,0:T(8,128)(2,1)} %g_hbm.1, bf16[768,128]{1,0:T(8,128)(2,1)} %wq_hbm.1, bf16[768,128]{1,0:T(8,128)(2,1)} %wk_hbm.1, bf16[768,128]{1,0:T(8,128)(2,1)} %wv_hbm.1, ...), custom_call_target="tpu_custom_call" | custom-call | tf_op jit(solution)/shard_map/tied_row_attention_grad/pallas_call | solution.py:453
  111.4 1.3 %convert_multiply_fusion = f32[2,256,768]{2,1,0:T(8,128)S(1)} fusion(bf16[2,256,768]{2,1,0:T(8,128)(2,1)} %get-tuple-element.8), kind=kLoop, calls=%fused_computation | loop fusion | flops 786432 | bytes 2359296 | tf_op jit(solution)/shard_map/mul | solution.py:502
  112.7 0.9 slice_bitcast_fusion
  113.6 0.0 copy-start
  113.6 0.9 copy.13
  114.5 0.9 copy.12
  115.4 0.9 copy.11
  116.3 0.0 copy-done
  116.3 0.9 copy.15
Async XLA Ops:
  113.6 2.7 %copy-start = (bf16[4,128,768]{2,1,0:T(8,128)(2,1)S(1)}, bf16[4,128,768]{2,1,0:T(8,128)(2,1)}, u32[]{:S(2)}) copy-start(bf16[4,128,768]{2,1,0:T(8,128)(2,1)} %get-tuple-element.23) | copy-start | bytes 2359300

commit v2 on v1

v2 whole, which is shorter than its diff:
```python
import math

import jax
import jax.numpy as jnp
from jax import lax
from jax.experimental import pallas as pl
from jax.experimental.pallas import tpu as pltpu
from jax.sharding import Mesh
from jax.sharding import PartitionSpec as P

AXES = ("y", "zh", "x", "zl", "core")
SEQ = ("y", "zh", "x")
HEAD = ("zl", "core")
ROWS, COLS, D, HEAD_DIM, HEADS = 4, 512, 768, 64, 2
WIDTH = HEADS * HEAD_DIM
ALL_ROWS = 256
C = 1.0 / (math.sqrt(HEAD_DIM) * math.sqrt(ALL_ROWS))
INV_ROOT = 1.0 / math.sqrt(ALL_ROWS * COLS)
COPIES = 176
F32, BF16 = jnp.float32, jnp.bfloat16


def nt(a, b):
    return lax.dot_general(a, b, (((1,), (1,)), ((), ())), preferred_element_type=F32)


def nn(a, b):
    return lax.dot_general(a, b, (((1,), (0,)), ((), ())), preferred_element_type=F32)


def tn(a, b):
    return lax.dot_general(a, b, (((0,), (0,)), ((), ())), preferred_element_type=F32)


class Copies:
    def __init__(self, send_sem, recv_sem):
        self.send_sem, self.recv_sem, self.made = send_sem, recv_sem, []

    def send(self, src, dst, device):
        k = len(self.made)
        copy = pltpu.make_async_remote_copy(
            src_ref=src,
            dst_ref=dst,
            send_sem=self.send_sem.at[k],
            recv_sem=self.recv_sem.at[k],
            device_id=device,
            device_id_type=pl.DeviceIdType.MESH,
        )
        copy.start()
        self.made.append(copy)
        return copy

    def drain(self):
        for copy in self.made:
            copy.wait_send()


class RingSum:
    def __init__(self, copies, piece, rel, rcv, tmp, right, left):
        self.copies, self.piece, self.rel, self.rcv, self.tmp = copies, piece, rel, rcv, tmp
        self.right, self.left = right, left

    def start_far(self):
        send, piece = self.copies.send, self.piece
        self.c1 = send(piece(2, 0), self.rel.at[0], self.right)
        self.c2 = send(piece(2, 1), self.rel.at[1], self.left)

    def start_near(self):
        send, piece = self.copies.send, self.piece
        self.c3 = send(piece(1, 1), self.rcv.at[0, 1], self.right)
        self.c4 = send(piece(3, 0), self.rcv.at[1, 0], self.left)

    def relay(self):
        send, piece = self.copies.send, self.piece
        self.c1.wait_recv()
        self.tmp[0] = (piece(1, 0)[...].astype(F32) + self.rel[0].astype(F32)).astype(BF16)
        self.c2.wait_recv()
        self.tmp[1] = (piece(3, 1)[...].astype(F32) + self.rel[1].astype(F32)).astype(BF16)
        self.c5 = send(self.tmp.at[0], self.rcv.at[0, 0], self.right)
        self.c6 = send(self.tmp.at[1], self.rcv.at[1, 1], self.left)

    def finish(self):
        for copy in (self.c3, self.c4, self.c5, self.c6):
            copy.wait_recv()
        return [
            self.piece(0, half)[...].astype(F32)
            + self.rcv[0, half].astype(F32)
            + self.rcv[1, half].astype(F32)
            for half in range(2)
        ]


class RingGather:
    def __init__(self, copies, block, right, left):
        self.copies, self.block, self.right, self.left = copies, block, right, left

    def start(self):
        whole = self.block(0, None)
        self.d1 = self.copies.send(whole, whole, self.right)
        self.d2 = self.copies.send(whole, whole, self.left)

    def relay(self):
        self.d1.wait_recv()
        far = self.block(3, 0)
        self.e1 = self.copies.send(far, far, self.right)
        self.d2.wait_recv()
        far = self.block(1, 1)
        self.e2 = self.copies.send(far, far, self.left)

    def finish(self):
        self.e1.wait_recv()
        self.e2.wait_recv()


def kernel(
    x_hbm, g_hbm, wq_hbm, wk_hbm, wv_hbm, wo_hbm,
    gin_ref, gq_ref, gk_ref, gv_ref, go_ref,
    xv, gv, wo, wfull, wt, proj, part,
    rel1, rcv1, tmp1, sum1, own1, rcv2, sum2, own2, rcv3,
    pd, att, grad, gall,
    wacc, wpart, wrcv1, wsum1, wrcv2, wrcv3, wfin,
    load_sem, send_sem, recv_sem,
):
    y, zh, x, zl, co = (lax.axis_index(n) for n in AXES)
    a = x * (1 - co) + y * co
    b = y * (1 - co) + x * co
    head = zl * 2 + co

    def dev(da=0, db=0, dc=0, dzl=0, dco=0):
        return (
            lax.rem(y + da * co + db * (1 - co), 4),
            lax.rem(zh + dc, 4),
            lax.rem(x + da * (1 - co) + db * co, 4),
            lax.rem(zl + dzl, 2),
            lax.rem(co + dco, 2),
        )

    a_to = [None] + [dev(da=k) for k in (1, 2, 3)]
    b_to = [None] + [dev(db=k) for k in (1, 2, 3)]
    z_to = [None] + [dev(dc=k) for k in (1, 2, 3)]
    h_core, h_chip, h_both = dev(dco=1), dev(dzl=1), dev(dzl=1, dco=1)
    near_first = (1, 3, 2)

    def rows_of(start, size):
        return pl.ds(pl.multiple_of(start, size), size)

    def place(at, off):
        return lax.rem(at + off, 4)

    mine = rows_of(head * WIDTH, WIDTH)
    loads = [
        pltpu.make_async_copy(w.at[...], wfull.at[t, :, mine], load_sem.at[t])
        for t, w in enumerate((wq_hbm, wk_hbm, wv_hbm))
    ]
    loads.append(pltpu.make_async_copy(x_hbm, xv, load_sem.at[3]))
    loads.append(pltpu.make_async_copy(wo_hbm, wo, load_sem.at[4]))
    loads.append(pltpu.make_async_copy(g_hbm, gv, load_sem.at[5]))
    for load in loads:
        load.start()

    barrier = pltpu.get_barrier_semaphore()
    friends = [*a_to[1:], *b_to[1:], *z_to[1:], h_core, h_chip, h_both]
    for friend in friends:
        pl.semaphore_signal(barrier, inc=1, device_id=friend, device_id_type=pl.DeviceIdType.MESH)

    copies = Copies(send_sem, recv_sem)
    for load in loads[:4]:
        load.wait()
    for t in range(3):
        wt[t * WIDTH : (t + 1) * WIDTH, :] = wfull[t, :, mine].T

    def project(r, _):
        res = nt(wt[...], xv[r]).astype(BF16)
        at = rows_of(r * HEAD_DIM, HEAD_DIM)
        for t in range(3):
            for h in range(HEADS):
                k = t * WIDTH + h * HEAD_DIM
                proj[t, h, at, :] = res[k : k + HEAD_DIM]
        return 0

    lax.fori_loop(0, ROWS, project, 0)

    def products(m, left, right):
        def one(k, _):
            h, blk = k // 4, lax.rem(k, 4)
            at = rows_of(blk * 128, 128)
            part[m, h, at, :] = tn(proj[left, h, :, at], proj[right, h]).astype(BF16)
            return 0

        lax.fori_loop(0, 4 * HEADS, one, 0)

    products(0, 0, 1)
    pl.semaphore_wait(barrier, len(friends))

    order = (2, 1, 3, 0)

    def ring1(m, k):
        def piece(off, half):
            return part.at[m, half, rows_of(place(a, off) * 128 + place(b, k) * 32, 32), :]

        return RingSum(copies, piece, rel1.at[m, k], rcv1.at[m, k], tmp1.at[m, k], a_to[1], a_to[3])

    first = [[ring1(m, k) for k in range(4)] for m in range(2)]

    def start_first(m):
        for k in order:
            first[m][k].start_far()
        for k in order:
            first[m][k].start_near()

    start_first(0)
    to_core = [copies.send(wfull.at[t, :, mine], wfull.at[t, :, mine], h_core) for t in range(3)]
    to_chip = [copies.send(wfull.at[t, :, mine], wfull.at[t, :, mine], h_chip) for t in range(3)]

    for load in loads[4:]:
        load.wait()

    def project_grad(r, _):
        res = nt(wo[...], gv[r]).astype(BF16)
        at = rows_of(r * HEAD_DIM, HEAD_DIM)
        for h in range(HEADS):
            proj[3, h, at, :] = res[h * HEAD_DIM : (h + 1) * HEAD_DIM]
        return 0

    lax.fori_loop(0, ROWS, project_grad, 0)
    for k in order:
        first[0][k].relay()
    products(1, 3, 2)
    start_first(1)

    second = [[None] * 4 for _ in range(2)]

    def end_first(m):
        for k in order:
            for half, total in enumerate(first[m][k].finish()):
                if k:
                    sum1[m, k - 1, half] = total.astype(BF16)
                else:
                    own1[m, half] = total
            if k:
                second[m][k] = copies.send(sum1.at[m, k - 1], rcv2.at[m, k - 1], b_to[k])

    def spot(off):
        at = place(zh, off)
        return at // 2, rows_of(lax.rem(at, 2) * 16, 16)

    third = [[None] * 4 for _ in range(2)]

    def end_second(m):
        total = own1[m]
        for k in near_first:
            second[m][k].wait_recv()
            total = total + rcv2[m, k - 1].astype(F32)
        sum2[m] = total.astype(BF16)
        own2[m] = total
        for k in (2, 1, 3):
            h, at = spot(k)
            third[m][k] = copies.send(sum2.at[m, h, at, :], rcv3.at[m, k - 1], z_to[k])

    end_first(0)
    for k in order:
        first[1][k].relay()
    end_second(0)
    end_first(1)

    theirs = rows_of((lax.rem(zl + 1, 2) * 2 + co) * WIDTH, WIDTH)
    forward = []
    for t in range(3):
        to_chip[t].wait_recv()
        forward.append(copies.send(wfull.at[t, :, theirs], wfull.at[t, :, theirs], h_core))
    end_second(1)

    def end_third(m):
        h, at = spot(0)
        total = own2[m, h, at, :]
        for k in near_first:
            third[m][k].wait_recv()
            total = total + rcv3[m, k - 1].astype(F32)
        return total

    exponent = jnp.exp(C * end_third(0))
    probs = exponent / jnp.sum(exponent, axis=1, keepdims=True)
    own_h, _ = spot(0)
    own_rows = rows_of(a * 128 + b * 32 + lax.rem(zh, 2) * 16, 16)
    pd[0, own_h, own_rows, :] = probs.astype(BF16)
    grad_probs = end_third(1)
    inner = jnp.sum(probs * grad_probs, axis=1, keepdims=True)
    pd[1, own_h, own_rows, :] = (C * probs * (grad_probs - inner)).astype(BF16)
    spread = [[], []]
    for m in range(2):
        own = pd.at[m, own_h, own_rows, :]
        spread[m] = [copies.send(own, own, z_to[k]) for k in (2, 1, 3)]

    def block(m, k):
        def at(off, half):
            rows = rows_of(place(a, off) * 128 + place(b, k) * 32, 32)
            return pd.at[m, :, rows, :] if half is None else pd.at[m, half, rows, :]

        return at

    gather_a = [
        [RingGather(copies, block(m, k), a_to[1], a_to[3]) for k in range(4)] for m in range(2)
    ]
    gather_b = [[None] * 4 for _ in range(2)]
    for m in range(2):
        for copy in spread[m]:
            copy.wait_recv()
        own = block(m, 0)(0, None)
        for k in (2, 1, 3):
            gather_b[m][k] = copies.send(own, own, b_to[k])
        gather_a[m][0].start()

    def pass_on(m, k):
        gather_b[m][(4 - k) % 4].wait_recv()
        gather_a[m][k].start()

    gather_a[0][0].relay()
    for m in range(2):
        for k in near_first:
            pass_on(m, k)
        if m == 0:
            gather_a[1][0].relay()
    for m in range(2):
        for k in near_first:
            gather_a[m][k].relay()

    def pair_value(h, _):
        p = pd[0, h]
        att[h] = nt(proj[2, h], p).astype(BF16).reshape(ROWS, HEAD_DIM, COLS)
        grad[2, h] = nn(proj[3, h], p).astype(BF16).reshape(ROWS, HEAD_DIM, COLS)
        return 0

    def pair_score(h, _):
        d = pd[1, h]
        grad[0, h] = nt(proj[1, h], d).astype(BF16).reshape(ROWS, HEAD_DIM, COLS)
        grad[1, h] = nn(proj[0, h], d).astype(BF16).reshape(ROWS, HEAD_DIM, COLS)
        return 0

    def to_heads(t):
        sent = []
        for device, dzl, dco in ((h_chip, 1, 0), (h_both, 1, 1), (h_core, 0, 1)):
            at = rows_of((lax.rem(zl + dzl, 2) * 2 + lax.rem(co + dco, 2)) * 128, 128)
            sent.append(copies.send(grad.at[t, :, :, :, at], gall.at[t, head], device))
        keep = pltpu.make_async_copy(grad.at[t, :, :, :, mine], gall.at[t, head], load_sem.at[6 + t])
        keep.start()
        return sent, keep

    def weight_part(p, kinds):
        def one(r, _):
            for k, (source, t) in enumerate(kinds):
                src = att if t is None else grad.at[t]
                lhs = jnp.concatenate([src[0, r], src[1, r]], axis=0)
                at = slice(k * WIDTH, (k + 1) * WIDTH)
                wacc[at, :] = jnp.where(r == 0, 0.0, wacc[at, :]) + nn(lhs, source[r])
            return 0

        lax.fori_loop(0, ROWS, one, 0)
        wpart[p] = wacc[...].astype(BF16)

    wfirst = [[None] * 4 for _ in range(2)]
    wsecond = [[None] * 4 for _ in range(2)]
    wthird = [[None] * 4 for _ in range(2)]

    def start_weights(p):
        for k in (2, 1, 3):
            wfirst[p][k] = copies.send(
                wpart.at[p, rows_of(place(a, k) * 64, 64), :], wrcv1.at[p, k - 1], a_to[k]
            )

    def end_wfirst(p):
        total = wpart[p, rows_of(a * 64, 64), :].astype(F32)
        for k in near_first:
            wfirst[p][k].wait_recv()
            total = total + wrcv1[p, k - 1].astype(F32)
        wsum1[p] = total.astype(BF16)
        for k in (2, 1, 3):
            wsecond[p][k] = copies.send(
                wsum1.at[p, rows_of(place(b, k) * 16, 16), :], wrcv2.at[p, k - 1], b_to[k]
            )

    def end_wsecond(p):
        total = wsum1[p, rows_of(b * 16, 16), :].astype(F32)
        for k in near_first:
            wsecond[p][k].wait_recv()
            total = total + wrcv2[p, k - 1].astype(F32)
        wrcv3[p, zh] = total.astype(BF16)
        own = wrcv3.at[p, zh]
        for k in (2, 1, 3):
            wthird[p][k] = copies.send(own, own, z_to[k])

    wgather_b = [[None] * 4 for _ in range(2)]
    wgather_a = [[], []]

    def wblock(p, k):
        return wfin.at[p, rows_of(a * 64 + place(b, k) * 16, 16), :]

    def spread_weights(p, k):
        own = wblock(p, k)
        for d in (2, 1, 3):
            wgather_a[p].append(copies.send(own, own, a_to[d]))

    def end_wthird(p):
        for k in near_first:
            wthird[p][k].wait_recv()
        total = wrcv3[p, 0].astype(F32) + wrcv3[p, 1].astype(F32)
        total = total + wrcv3[p, 2].astype(F32) + wrcv3[p, 3].astype(F32)
        wfin[p, rows_of(a * 64 + b * 16, 16), :] = total.astype(BF16)
        own = wblock(p, 0)
        for k in (2, 1, 3):
            wgather_b[p][k] = copies.send(own, own, b_to[k])
        spread_weights(p, 0)

    def pass_on_weights(p):
        for k in near_first:
            wgather_b[p][(4 - k) % 4].wait_recv()
            spread_weights(p, k)

    for k in range(4):
        gather_a[0][k].finish()
    lax.fori_loop(0, HEADS, pair_value, 0)
    moved = {2: to_heads(2)}
    weight_part(0, ((xv, 2), (gv, None)))
    start_weights(0)
    for k in range(4):
        gather_a[1][k].finish()
    lax.fori_loop(0, HEADS, pair_score, 0)
    moved[0] = to_heads(0)
    moved[1] = to_heads(1)
    weight_part(1, ((xv, 0), (xv, 1)))
    start_weights(1)
    end_wfirst(0)
    end_wsecond(0)
    end_wfirst(1)
    end_wsecond(1)
    end_wthird(0)
    pass_on_weights(0)
    end_wthird(1)

    for copy in to_core + forward:
        copy.wait_recv()
    for t in range(3):
        sent, keep = moved[t]
        keep.wait()
        for copy in sent:
            copy.wait_recv()
    pass_on_weights(1)

    def block_inputs(k, _):
        r = k * 2
        total = None
        for t in range(3):
            sides = [
                jnp.concatenate([gall[t, hd, h, r + s] for hd in range(4) for h in range(HEADS)], axis=0)
                for s in range(2)
            ]
            term = nn(wfull[t], jnp.concatenate(sides, axis=1))
            total = term if total is None else total + term
        flat = total.T.astype(BF16)
        gin_ref[r] = flat[:128]
        gin_ref[r + 1] = flat[128:]
        return 0

    lax.fori_loop(0, 2, block_inputs, 0)
    for p in range(2):
        for copy in wgather_a[p]:
            copy.wait_recv()
    gv_ref[...] = wfin[0, :WIDTH].T
    go_ref[...] = wfin[0, WIDTH:]
    gq_ref[...] = wfin[1, :WIDTH].T
    gk_ref[...] = wfin[1, WIDTH:].T
    copies.drain()


def body(inputs, out_grad, w_query, w_key, w_value, w_output):
    vmem = lambda *shape: pltpu.VMEM(shape, BF16)
    gin, gq, gk, gv, go = pl.pallas_call(
        kernel,
        out_shape=(
            jax.ShapeDtypeStruct((ROWS, 128, D), BF16),
            *(jax.ShapeDtypeStruct((D, WIDTH), BF16) for _ in range(3)),
            jax.ShapeDtypeStruct((WIDTH, D), BF16),
        ),
        in_specs=[pl.BlockSpec(memory_space=pl.ANY)] * 6,
        out_specs=(pl.BlockSpec(memory_space=pltpu.VMEM),) * 5,
        scratch_shapes=[
            vmem(ROWS, COLS, D),
            vmem(ROWS, COLS, D),
            vmem(WIDTH, D),
            vmem(3, D, 4 * WIDTH),
            vmem(3 * WIDTH, D),
            vmem(4, HEADS, ROWS * HEAD_DIM, COLS),
            vmem(2, HEADS, COLS, COLS),
            vmem(2, 4, 2, 32, COLS),
            vmem(2, 4, 2, 2, 32, COLS),
            vmem(2, 4, 2, 32, COLS),
            vmem(2, 3, HEADS, 32, COLS),
            pltpu.VMEM((2, HEADS, 32, COLS), F32),
            vmem(2, 3, HEADS, 32, COLS),
            vmem(2, HEADS, 32, COLS),
            pltpu.VMEM((2, HEADS, 32, COLS), F32),
            vmem(2, 3, 16, COLS),
            vmem(2, HEADS, COLS, COLS),
            vmem(HEADS, ROWS, HEAD_DIM, COLS),
            vmem(3, HEADS, ROWS, HEAD_DIM, COLS),
            vmem(3, 4, HEADS, ROWS, HEAD_DIM, 128),
            pltpu.VMEM((2 * WIDTH, D), F32),
            vmem(2, 2 * WIDTH, D),
            vmem(2, 3, 64, D),
            vmem(2, 64, D),
            vmem(2, 3, 16, D),
            vmem(2, 4, 16, D),
            vmem(2, 2 * WIDTH, D),
            pltpu.SemaphoreType.DMA((9,)),
            pltpu.SemaphoreType.DMA((COPIES,)),
            pltpu.SemaphoreType.DMA((COPIES,)),
        ],
        compiler_params=pltpu.CompilerParams(
            collective_id=0, has_side_effects=True, vmem_limit_bytes=56 * 1024 * 1024
        ),
        name="tied_row_attention_grad",
    )(inputs, out_grad, w_query, w_key, w_value, w_output)
    scaled = lambda w: w.astype(F32) * INV_ROOT
    return gin, scaled(gq), scaled(gk), scaled(gv), scaled(go)


def solution(mesh):
    finer = Mesh(mesh.devices.reshape(4, 4, 4, 2, 2), AXES)
    return jax.shard_map(
        body,
        mesh=finer,
        in_specs=(
            P(SEQ, None, None),
            P(SEQ, None, None),
            P(None, HEAD),
            P(None, HEAD),
            P(None, HEAD),
            P(HEAD, None),
        ),
        out_specs=(
            P(SEQ, HEAD, None),
            P(None, HEAD),
            P(None, HEAD),
            P(None, HEAD),
            P(HEAD, None),
        ),
        check_vma=False,
    )
```

time: 117 us -> 100 us (0.85)
  Pallas kernels: 111 us -> 91.9 us
  other arithmetic: 1.26 us -> 5.36 us
  local copies, waits for them, and re-layouts: 4.52 us -> 2.06 us
    pallas_call x1, Pallas kernels: 111 us -> 91.9 us  [body(): pl.pallas_call(kernel, out_shape=(jax.ShapeDtypeStruct((ROWS, 128, D), BF...]
    mul x1 -> x3, other arithmetic: 1.26 us -> 5.36 us  [body(): scaled = lambda w: w.astype(F32) * INV_ROOT]
    unnamed x6 -> x1, local copies, waits for them, and re-layouts: 3.62 us -> 2.06 us
where the time goes in v2:
time: 100 us; the launch traced here: 99.9 us
  Pallas kernels  91.9 us (92%)
  other arithmetic  5.36 us (5%)
  local copies, waits for them, and re-layouts  2.06 us (2%)
    pallas_call x1, Pallas kernels, body(): pl.pallas_call(kernel, out_shape=(jax.ShapeDtypeStruct((ROWS, 128, D), BF...  91.9 us
    mul x3, other arithmetic, body(): scaled = lambda w: w.astype(F32) * INV_ROOT  5.36 us
    unnamed x1, local copies, waits for them, and re-layouts  2.06 us

profile of v2, /device:TPU:2, one launch (start us, length us, event | category | flops | bytes accessed | tf_op | source)
XLA Modules:
  0.0 99.9 jit_solution(6694707221325023376)
XLA Ops:
  0.6 91.9 %tied_row_attention_grad.1 = (bf16[4,128,768]{2,1,0:T(8,128)(2,1)}, bf16[768,128]{1,0:T(8,128)(2,1)}, bf16[768,128]{1,0:T(8,128)(2,1)}, bf16[768,128]{1,0:T(8,128)(2,1)}, bf16[128,768]{1,0:T(8,128)(2,1)}) custom-call(bf16[4,512,768]{2,1,0:T(8,128)(2,1)} %x_hbm.1, bf16[4,512,768]{2,1,0:T(8,128)(2,1)} %g_hbm.1, bf16[768,128]{1,0:T(8,128)(2,1)} %wq_hbm.1, ...), custom_call_target="tpu_custom_call" | custom-call | tf_op jit(solution)/shard_map/tied_row_attention_grad/pallas_call | solution.py:476
  92.5 1.7 %convert_multiply_fusion.3 = f32[768,128]{1,0:T(8,128)} fusion(bf16[768,128]{1,0:T(8,128)(2,1)} %get-tuple-element.11), kind=kLoop, calls=%fused_computation.3 | loop fusion | flops 196608 | bytes 589824 | tf_op jit(solution)/shard_map/mul | solution.py:522
  94.2 2.0 %convert_multiply_fusion.1 = (f32[768,128]{1,0:T(8,128)}, f32[768,128]{1,0:T(8,128)}) fusion(bf16[768,128]{1,0:T(8,128)(2,1)} %get-tuple-element.13, bf16[768,128]{1,0:T(8,128)(2,1)} %get-tuple-element.12), kind=kLoop, calls=%fused_computation.1 | loop fusion | flops 393216 | bytes 1179648 | tf_op jit(solution)/shard_map/mul | solution.py:522
  96.2 1.7 %convert_multiply_fusion = f32[128,768]{1,0:T(8,128)} fusion(bf16[128,768]{1,0:T(8,128)(2,1)} %get-tuple-element.14), kind=kLoop, calls=%fused_computation | loop fusion | flops 196608 | bytes 589824 | tf_op jit(solution)/shard_map/mul | solution.py:522
  97.9 2.1 %copy.12 = bf16[4,128,768]{2,1,0:T(8,128)(2,1)} copy(bf16[4,128,768]{2,1,0:T(8,128)(2,1)} %get-tuple-element.22) | data formatting | bytes 1572864

commit v3 on v2

--- a/solution.py
+++ b/solution.py
@@ -155,7 +155,7 @@
     loads.append(pltpu.make_async_copy(x_hbm, xv, load_sem.at[3]))
     loads.append(pltpu.make_async_copy(wo_hbm, wo, load_sem.at[4]))
     loads.append(pltpu.make_async_copy(g_hbm, gv, load_sem.at[5]))
-    for load in loads:
+    for load in loads[:4]:
         load.start()
 
     barrier = pltpu.get_barrier_semaphore()
@@ -164,10 +164,14 @@
         pl.semaphore_signal(barrier, inc=1, device_id=friend, device_id_type=pl.DeviceIdType.MESH)
 
     copies = Copies(send_sem, recv_sem)
-    for load in loads[:4]:
+    for load in loads[:3]:
         load.wait()
+    for load in loads[4:]:
+        load.start()
     for t in range(3):
         wt[t * WIDTH : (t + 1) * WIDTH, :] = wfull[t, :, mine].T
+
+    loads[3].wait()
 
     def project(r, _):
         res = nt(wt[...], xv[r]).astype(BF16)
@@ -209,9 +213,6 @@
             first[m][k].start_near()
 
     start_first(0)
-    to_core = [copies.send(wfull.at[t, :, mine], wfull.at[t, :, mine], h_core) for t in range(3)]
-    to_chip = [copies.send(wfull.at[t, :, mine], wfull.at[t, :, mine], h_chip) for t in range(3)]
-
     for load in loads[4:]:
         load.wait()
 
@@ -263,11 +264,6 @@
     end_second(0)
     end_first(1)
 
-    theirs = rows_of((lax.rem(zl + 1, 2) * 2 + co) * WIDTH, WIDTH)
-    forward = []
-    for t in range(3):
-        to_chip[t].wait_recv()
-        forward.append(copies.send(wfull.at[t, :, theirs], wfull.at[t, :, theirs], h_core))
     end_second(1)
 
     def end_third(m):
@@ -310,6 +306,9 @@
             gather_b[m][k] = copies.send(own, own, b_to[k])
         gather_a[m][0].start()
 
+    to_core = [copies.send(wfull.at[t, :, mine], wfull.at[t, :, mine], h_core) for t in range(3)]
+    to_chip = [copies.send(wfull.at[t, :, mine], wfull.at[t, :, mine], h_chip) for t in range(3)]
+
     def pass_on(m, k):
         gather_b[m][(4 - k) % 4].wait_recv()
         gather_a[m][k].start()
@@ -415,6 +414,11 @@
             wgather_b[p][(4 - k) % 4].wait_recv()
             spread_weights(p, k)
 
+    theirs = rows_of((lax.rem(zl + 1, 2) * 2 + co) * WIDTH, WIDTH)
+    forward = []
+    for t in range(3):
+        to_chip[t].wait_recv()
+        forward.append(copies.send(wfull.at[t, :, theirs], wfull.at[t, :, theirs], h_core))
     for k in range(4):
         gather_a[0][k].finish()
     lax.fori_loop(0, HEADS, pair_value, 0)
@@ -471,6 +475,21 @@
     copies.drain()
 
 
+def last_step(*refs):
+    sources, outs, held, made, sem = refs[:5], refs[5:10], refs[10:15], refs[15:19], refs[19]
+    into = [pltpu.make_async_copy(sources[k], held[k], sem.at[k]) for k in range(5)]
+    back = [pltpu.make_async_copy(held[0] if k == 0 else made[k - 1], outs[k], sem.at[5 + k]) for k in range(5)]
+    for copy in into:
+        copy.start()
+    for k in range(5):
+        into[k].wait()
+        if k:
+            made[k - 1][...] = held[k][...].astype(F32) * INV_ROOT
+        back[k].start()
+    for copy in back:
+        copy.wait()
+
+
 def body(inputs, out_grad, w_query, w_key, w_value, w_output):
     vmem = lambda *shape: pltpu.VMEM(shape, BF16)
     gin, gq, gk, gv, go = pl.pallas_call(
@@ -480,7 +499,7 @@
             *(jax.ShapeDtypeStruct((D, WIDTH), BF16) for _ in range(3)),
             jax.ShapeDtypeStruct((WIDTH, D), BF16),
         ),
-        in_specs=[pl.BlockSpec(memory_space=pl.ANY)] * 6,
+        in_specs=[pl.BlockSpec(memory_space=pltpu.HBM)] * 6,
         out_specs=(pl.BlockSpec(memory_space=pltpu.VMEM),) * 5,
         scratch_shapes=[
             vmem(ROWS, COLS, D),
@@ -519,8 +538,26 @@
         ),
         name="tied_row_attention_grad",
     )(inputs, out_grad, w_query, w_key, w_value, w_output)
-    scaled = lambda w: w.astype(F32) * INV_ROOT
-    return gin, scaled(gq), scaled(gk), scaled(gv), scaled(go)
+    return pl.pallas_call(
+        last_step,
+        out_shape=(
+            jax.ShapeDtypeStruct((ROWS, 128, D), BF16),
+            *(jax.ShapeDtypeStruct((D, WIDTH), F32) for _ in range(3)),
+            jax.ShapeDtypeStruct((WIDTH, D), F32),
+        ),
+        in_specs=[pl.BlockSpec(memory_space=pl.ANY)] * 5,
+        out_specs=(pl.BlockSpec(memory_space=pl.ANY),) * 5,
+        scratch_shapes=[
+            vmem(ROWS, 128, D),
+            *(vmem(D, WIDTH) for _ in range(3)),
+            vmem(WIDTH, D),
+            *(pltpu.VMEM((D, WIDTH), F32) for _ in range(3)),
+            pltpu.VMEM((WIDTH, D), F32),
+            pltpu.SemaphoreType.DMA((10,)),
+        ],
+        compiler_params=pltpu.CompilerParams(vmem_limit_bytes=60 * 1024 * 1024),
+        name="scale_weight_grads",
+    )(gin, gq, gk, gv, go)
 
 
 def solution(mesh):

time: 100 us -> 95.5 us (0.955)
  other arithmetic: 5.36 us -> 0 us
  Pallas kernels: 91.9 us -> 94.5 us
  local copies, waits for them, and re-layouts: 2.06 us -> 0 us
    mul x3 -> x0, other arithmetic: 5.36 us -> none  [body(): scaled = lambda w: w.astype(F32) * INV_ROOT]
    pallas_call x0 -> x1, Pallas kernels: none -> 2.61 us  [body(): pl.pallas_call(last_step, out_shape=(jax.ShapeDtypeStruct((ROWS, 128, D),...]
    unnamed x1 -> x0, local copies, waits for them, and re-layouts: 2.06 us -> none
where the time goes in v3:
time: 95.5 us; the launch traced here: 95.1 us
  Pallas kernels  94.5 us (99%)
    pallas_call x1, Pallas kernels, body(): pl.pallas_call(kernel, out_shape=(jax.ShapeDtypeStruct((ROWS, 128, D), BF...  91.9 us
    pallas_call x1, Pallas kernels, body(): pl.pallas_call(last_step, out_shape=(jax.ShapeDtypeStruct((ROWS, 128, D),...  2.61 us

profile of v3, /device:TPU:2, one launch (start us, length us, event | category | flops | bytes accessed | tf_op | source)
XLA Modules:
  0.0 95.1 jit_solution(10229259483430196818)
XLA Ops:
  0.6 91.9 %tied_row_attention_grad.1 = (bf16[4,128,768]{2,1,0:T(8,128)(2,1)}, bf16[768,128]{1,0:T(8,128)(2,1)}, bf16[768,128]{1,0:T(8,128)(2,1)}, bf16[768,128]{1,0:T(8,128)(2,1)}, bf16[128,768]{1,0:T(8,128)(2,1)}) custom-call(bf16[4,512,768]{2,1,0:T(8,128)(2,1)} %x_hbm.1, bf16[4,512,768]{2,1,0:T(8,128)(2,1)} %g_hbm.1, bf16[768,128]{1,0:T(8,128)(2,1)} %wq_hbm.1, ...), custom_call_target="tpu_custom_call" | custom-call | tf_op jit(solution)/shard_map/tied_row_attention_grad/pallas_call | solution.py:495
  92.5 2.6 %scale_weight_grads.1 = (bf16[4,128,768]{2,1,0:T(8,128)(2,1)}, f32[768,128]{1,0:T(8,128)}, f32[768,128]{1,0:T(8,128)}, f32[768,128]{1,0:T(8,128)}, f32[128,768]{1,0:T(8,128)}) custom-call(bf16[4,128,768]{2,1,0:T(8,128)(2,1)} %get-tuple-element.10.refs_0_, bf16[768,128]{1,0:T(8,128)(2,1)} %get-tuple-element.11.refs_1_, ...), custom_call_target="tpu_custom_call" | custom-call | tf_op jit(solution)/shard_map/scale_weight_grads/pallas_call | solution.py:541

commit v4 on v3

--- a/solution.py
+++ b/solution.py
@@ -148,15 +148,13 @@
         return lax.rem(at + off, 4)
 
     mine = rows_of(head * WIDTH, WIDTH)
-    loads = [
-        pltpu.make_async_copy(w.at[...], wfull.at[t, :, mine], load_sem.at[t])
-        for t, w in enumerate((wq_hbm, wk_hbm, wv_hbm))
-    ]
-    loads.append(pltpu.make_async_copy(x_hbm, xv, load_sem.at[3]))
-    loads.append(pltpu.make_async_copy(wo_hbm, wo, load_sem.at[4]))
-    loads.append(pltpu.make_async_copy(g_hbm, gv, load_sem.at[5]))
-    for load in loads[:4]:
-        load.start()
+    load = lambda src, dst, k: pltpu.make_async_copy(src, dst, load_sem.at[k])
+    load_w = [load(w.at[...], wfull.at[t, :, mine], t) for t, w in enumerate((wq_hbm, wk_hbm, wv_hbm))]
+    load_x = [load(x_hbm.at[r], xv.at[r], 3 + r) for r in range(ROWS)]
+    load_g = [load(g_hbm.at[r], gv.at[r], 7 + r) for r in range(ROWS)]
+    load_o = load(wo_hbm, wo, 11)
+    for copy in (load_w[0], load_w[1], *load_x):
+        copy.start()
 
     barrier = pltpu.get_barrier_semaphore()
     friends = [*a_to[1:], *b_to[1:], *z_to[1:], h_core, h_chip, h_both]
@@ -164,37 +162,33 @@
         pl.semaphore_signal(barrier, inc=1, device_id=friend, device_id_type=pl.DeviceIdType.MESH)
 
     copies = Copies(send_sem, recv_sem)
-    for load in loads[:3]:
-        load.wait()
-    for load in loads[4:]:
-        load.start()
-    for t in range(3):
+    def turn(t):
+        load_w[t].wait()
         wt[t * WIDTH : (t + 1) * WIDTH, :] = wfull[t, :, mine].T
 
-    loads[3].wait()
-
-    def project(r, _):
-        res = nt(wt[...], xv[r]).astype(BF16)
+    def keep_projection(res, t, r):
         at = rows_of(r * HEAD_DIM, HEAD_DIM)
-        for t in range(3):
-            for h in range(HEADS):
-                k = t * WIDTH + h * HEAD_DIM
-                proj[t, h, at, :] = res[k : k + HEAD_DIM]
-        return 0
-
-    lax.fori_loop(0, ROWS, project, 0)
-
-    def products(m, left, right):
-        def one(k, _):
-            h, blk = k // 4, lax.rem(k, 4)
-            at = rows_of(blk * 128, 128)
+        for h in range(HEADS):
+            proj[t, h, at, :] = res[h * HEAD_DIM : (h + 1) * HEAD_DIM].astype(BF16)
+
+    turn(0)
+    turn(1)
+    for r in range(ROWS):
+        load_x[r].wait()
+        res = nt(wt[: 2 * WIDTH, :], xv[r])
+        keep_projection(res[:WIDTH], 0, r)
+        keep_projection(res[WIDTH:], 1, r)
+    for copy in (load_w[2], load_o, *load_g):
+        copy.start()
+
+    def products(m, left, right, off):
+        at = rows_of(place(a, off) * 128, 128)
+
+        def one(h, _):
             part[m, h, at, :] = tn(proj[left, h, :, at], proj[right, h]).astype(BF16)
             return 0
 
-        lax.fori_loop(0, 4 * HEADS, one, 0)
-
-    products(0, 0, 1)
-    pl.semaphore_wait(barrier, len(friends))
+        lax.fori_loop(0, HEADS, one, 0)
 
     order = (2, 1, 3, 0)
 
@@ -206,28 +200,33 @@
 
     first = [[ring1(m, k) for k in range(4)] for m in range(2)]
 
-    def start_first(m):
+    def start_first(m, left, right):
+        products(m, left, right, 2)
+        products(m, left, right, 1)
+        if m == 0:
+            pl.semaphore_wait(barrier, len(friends))
         for k in order:
             first[m][k].start_far()
+        products(m, left, right, 3)
+        products(m, left, right, 0)
         for k in order:
             first[m][k].start_near()
 
-    start_first(0)
-    for load in loads[4:]:
-        load.wait()
-
-    def project_grad(r, _):
-        res = nt(wo[...], gv[r]).astype(BF16)
-        at = rows_of(r * HEAD_DIM, HEAD_DIM)
-        for h in range(HEADS):
-            proj[3, h, at, :] = res[h * HEAD_DIM : (h + 1) * HEAD_DIM]
+    start_first(0, 0, 1)
+    turn(2)
+    load_o.wait()
+    for copy in load_g:
+        copy.wait()
+
+    def project_rest(r, _):
+        keep_projection(nt(wt[2 * WIDTH :, :], xv[r]), 2, r)
+        keep_projection(nt(wo[...], gv[r]), 3, r)
         return 0
 
-    lax.fori_loop(0, ROWS, project_grad, 0)
+    lax.fori_loop(0, ROWS, project_rest, 0)
     for k in order:
         first[0][k].relay()
-    products(1, 3, 2)
-    start_first(1)
+    start_first(1, 3, 2)
 
     second = [[None] * 4 for _ in range(2)]
 
@@ -319,9 +318,8 @@
             pass_on(m, k)
         if m == 0:
             gather_a[1][0].relay()
-    for m in range(2):
-        for k in near_first:
-            gather_a[m][k].relay()
+    for m, k in ((0, 1), (0, 3), (0, 2), (1, 1), (1, 3)):
+        gather_a[m][k].relay()
 
     def pair_value(h, _):
         p = pd[0, h]
@@ -340,7 +338,7 @@
         for device, dzl, dco in ((h_chip, 1, 0), (h_both, 1, 1), (h_core, 0, 1)):
             at = rows_of((lax.rem(zl + dzl, 2) * 2 + lax.rem(co + dco, 2)) * 128, 128)
             sent.append(copies.send(grad.at[t, :, :, :, at], gall.at[t, head], device))
-        keep = pltpu.make_async_copy(grad.at[t, :, :, :, mine], gall.at[t, head], load_sem.at[6 + t])
+        keep = pltpu.make_async_copy(grad.at[t, :, :, :, mine], gall.at[t, head], load_sem.at[12 + t])
         keep.start()
         return sent, keep
 
@@ -414,14 +412,15 @@
             wgather_b[p][(4 - k) % 4].wait_recv()
             spread_weights(p, k)
 
+    for k in range(4):
+        gather_a[0][k].finish()
+    lax.fori_loop(0, HEADS, pair_value, 0)
+    gather_a[1][2].relay()
     theirs = rows_of((lax.rem(zl + 1, 2) * 2 + co) * WIDTH, WIDTH)
     forward = []
     for t in range(3):
         to_chip[t].wait_recv()
         forward.append(copies.send(wfull.at[t, :, theirs], wfull.at[t, :, theirs], h_core))
-    for k in range(4):
-        gather_a[0][k].finish()
-    lax.fori_loop(0, HEADS, pair_value, 0)
     moved = {2: to_heads(2)}
     weight_part(0, ((xv, 2), (gv, None)))
     start_weights(0)
@@ -529,7 +528,7 @@
             vmem(2, 3, 16, D),
             vmem(2, 4, 16, D),
             vmem(2, 2 * WIDTH, D),
-            pltpu.SemaphoreType.DMA((9,)),
+            pltpu.SemaphoreType.DMA((15,)),
             pltpu.SemaphoreType.DMA((COPIES,)),
             pltpu.SemaphoreType.DMA((COPIES,)),
         ],

time: 95.5 us -> 94.5 us (0.990)
  no operation moved by 1% of the time
where the time goes in v4:
time: 94.5 us; the launch traced here: 94.4 us
  Pallas kernels  93.8 us (99%)
    pallas_call x1, Pallas kernels, body(): pl.pallas_call(kernel, out_shape=(jax.ShapeDtypeStruct((ROWS, 128, D), BF...  91.1 us
    pallas_call x1, Pallas kernels, body(): pl.pallas_call(last_step, out_shape=(jax.ShapeDtypeStruct((ROWS, 128, D),...  2.61 us

profile of v4, /device:TPU:2, one launch (start us, length us, event | category | flops | bytes accessed | tf_op | source)
XLA Modules:
  0.0 94.4 jit_solution(18057674936081349696)
XLA Ops:
  0.6 91.1 %tied_row_attention_grad.1 = (bf16[4,128,768]{2,1,0:T(8,128)(2,1)}, bf16[768,128]{1,0:T(8,128)(2,1)}, bf16[768,128]{1,0:T(8,128)(2,1)}, bf16[768,128]{1,0:T(8,128)(2,1)}, bf16[128,768]{1,0:T(8,128)(2,1)}) custom-call(bf16[4,512,768]{2,1,0:T(8,128)(2,1)} %x_hbm.1, bf16[4,512,768]{2,1,0:T(8,128)(2,1)} %g_hbm.1, bf16[768,128]{1,0:T(8,128)(2,1)} %wq_hbm.1, ...), custom_call_target="tpu_custom_call" | custom-call | tf_op jit(solution)/shard_map/tied_row_attention_grad/pallas_call | solution.py:494
  91.8 2.6 %scale_weight_grads.1 = (bf16[4,128,768]{2,1,0:T(8,128)(2,1)}, f32[768,128]{1,0:T(8,128)}, f32[768,128]{1,0:T(8,128)}, f32[768,128]{1,0:T(8,128)}, f32[128,768]{1,0:T(8,128)}) custom-call(bf16[4,128,768]{2,1,0:T(8,128)(2,1)} %get-tuple-element.10.refs_0_, bf16[768,128]{1,0:T(8,128)(2,1)} %get-tuple-element.11.refs_1_, ...), custom_call_target="tpu_custom_call" | custom-call | tf_op jit(solution)/shard_map/scale_weight_grads/pallas_call | solution.py:540

commit v5 on v4

--- a/solution.py
+++ b/solution.py
@@ -278,13 +278,16 @@
     own_h, _ = spot(0)
     own_rows = rows_of(a * 128 + b * 32 + lax.rem(zh, 2) * 16, 16)
     pd[0, own_h, own_rows, :] = probs.astype(BF16)
+
+    def to_third(m):
+        own = pd.at[m, own_h, own_rows, :]
+        return [copies.send(own, own, z_to[k]) for k in (2, 1, 3)]
+
+    spread = [to_third(0)]
     grad_probs = end_third(1)
     inner = jnp.sum(probs * grad_probs, axis=1, keepdims=True)
     pd[1, own_h, own_rows, :] = (C * probs * (grad_probs - inner)).astype(BF16)
-    spread = [[], []]
-    for m in range(2):
-        own = pd.at[m, own_h, own_rows, :]
-        spread[m] = [copies.send(own, own, z_to[k]) for k in (2, 1, 3)]
+    spread.append(to_third(1))
 
     def block(m, k):
         def at(off, half):

time: 94.5 us -> 91.2 us (0.965)
  Pallas kernels: 93.8 us -> 90.5 us
    pallas_call x1, Pallas kernels: 91.1 us -> 87.9 us  [body(): pl.pallas_call(kernel, out_shape=(jax.ShapeDtypeStruct((ROWS, 128, D), BF...]
where the time goes in v5:
time: 91.2 us; the launch traced here: 91.1 us
  Pallas kernels  90.5 us (99%)
    pallas_call x1, Pallas kernels, body(): pl.pallas_call(kernel, out_shape=(jax.ShapeDtypeStruct((ROWS, 128, D), BF...  87.9 us
    pallas_call x1, Pallas kernels, body(): pl.pallas_call(last_step, out_shape=(jax.ShapeDtypeStruct((ROWS, 128, D),...  2.61 us

profile of v5, /device:TPU:2, one launch (start us, length us, event | category | flops | bytes accessed | tf_op | source)
XLA Modules:
  0.0 91.1 jit_solution(16952440423344069058)
XLA Ops:
  0.6 87.9 %tied_row_attention_grad.1 = (bf16[4,128,768]{2,1,0:T(8,128)(2,1)}, bf16[768,128]{1,0:T(8,128)(2,1)}, bf16[768,128]{1,0:T(8,128)(2,1)}, bf16[768,128]{1,0:T(8,128)(2,1)}, bf16[128,768]{1,0:T(8,128)(2,1)}) custom-call(bf16[4,512,768]{2,1,0:T(8,128)(2,1)} %x_hbm.1, bf16[4,512,768]{2,1,0:T(8,128)(2,1)} %g_hbm.1, bf16[768,128]{1,0:T(8,128)(2,1)} %wq_hbm.1, ...), custom_call_target="tpu_custom_call" | custom-call | tf_op jit(solution)/shard_map/tied_row_attention_grad/pallas_call | solution.py:497
  88.5 2.6 %scale_weight_grads.1 = (bf16[4,128,768]{2,1,0:T(8,128)(2,1)}, f32[768,128]{1,0:T(8,128)}, f32[768,128]{1,0:T(8,128)}, f32[768,128]{1,0:T(8,128)}, f32[128,768]{1,0:T(8,128)}) custom-call(bf16[4,128,768]{2,1,0:T(8,128)(2,1)} %get-tuple-element.10.refs_0_, bf16[768,128]{1,0:T(8,128)(2,1)} %get-tuple-element.11.refs_1_, ...), custom_call_target="tpu_custom_call" | custom-call | tf_op jit(solution)/shard_map/scale_weight_grads/pallas_call | solution.py:543
